TPU v7x, 32 devices: a whole 2x2x4 slice. The times are simulated.
32 devices in a mesh: slab: 4 (over y, x), energy: 8 (over z, core).
Axes of the slice: x: 2, y: 2, z: 4, core: 2. Of those that a mesh axis runs over, the one named last changes fastest.
Arguments:
- inverse_blocks: float32 [16, 16, 2, 256, 256], P('energy', 'slab'), as said below
- couplings: float32 [16, 16, 2, 256, 256], P('energy', 'slab'), as said below
- lead_column: float32 [16, 2, 256, 256], P('energy'), may hold values from -6 to 6
- w_table: float32 [2, 16383], replicated, may hold values from -1.05 to 1.05
- energy_index: int32 [16], replicated, may hold values from 0 to 8191
Outputs:
- green_column: float32 [16, 16, 2, 256, 256], P('energy', 'slab')
- self_energy: float32 [16, 16, 2, 256, 256], P(None, 'slab', None, 'energy')
Inputs may be any that keep to these rules, and one draw needn't show every extreme that they name: `inverse_blocks`: the inverse blocks and couplings each have a diagonal of modulus near 0.95 with random phases and independent off-diagonal entries. `couplings`: as for inverse_blocks, drawn independently.
All inputs are finite; a program needn't handle non-finite values.
Results may differ from a plain program's by a relative error of at most 0.00014.
Values sent between devices are 32-bit elements; how exact they have to be, the bound alone decides.
No kernel may reach another device: no remote copies, remote signals or barrier semaphores. Data moves between devices by JAX's collectives and lax.ppermute only.
A program may use at most 128 MiB of HBM per device.

v0:
```python
import functools

import jax
import jax.numpy as jnp
from jax import lax
from jax.experimental import pallas as pl
from jax.experimental.pallas import tpu as pltpu
from jax.sharding import PartitionSpec as P


F32 = jnp.float32
BF16 = jnp.bfloat16
SUBLANES = 8


def split(x):
    high = x.astype(BF16)
    return high, (x - high.astype(F32)).astype(BF16)


def dot3(left, right):
    def dot(a, b):
        return jnp.dot(a, b, preferred_element_type=F32)

    return dot(left[0], right[0]) + (dot(left[0], right[1]) + dot(left[1], right[0]))


def left_parts(real, imag):
    return split(real + imag), split(real), split(imag)


def right_parts(real, imag):
    return split(real), split(imag - real), split(real + imag)


def complex_product(left, right):
    first = dot3(left[0], right[0])
    second = dot3(left[1], right[1])
    third = dot3(left[2], right[2])
    return first - third, first + second


def prefix_kernel(g_ref, h_ref, p_ref, q_ref):
    block = pl.program_id(0)
    real, imag = complex_product(
        left_parts(g_ref[0, 0, 0], g_ref[0, 0, 1]), right_parts(h_ref[0, 0, 0], h_ref[0, 0, 1])
    )
    real, imag = -real, -imag

    @pl.when(block == 0)
    def _():
        q_ref[0] = real
        q_ref[1] = imag

    @pl.when(block > 0)
    def _():
        re, im = complex_product(left_parts(real, imag), right_parts(q_ref[0], q_ref[1]))
        q_ref[0] = re
        q_ref[1] = im

    p_ref[0] = q_ref[...]


def prefixes(inverse_blocks, couplings, energy):
    _, blocks, _, size, _ = inverse_blocks.shape
    spec = pl.BlockSpec((1, 1, 2, size, size), lambda k: (energy, k, 0, 0, 0))
    return pl.pallas_call(
        prefix_kernel,
        grid=(blocks,),
        in_specs=[spec, spec],
        out_specs=[
            pl.BlockSpec((1, 2, size, size), lambda k: (k, 0, 0, 0)),
            pl.BlockSpec((2, size, size), lambda k: (0, 0, 0)),
        ],
        out_shape=[
            jax.ShapeDtypeStruct((blocks, 2, size, size), F32),
            jax.ShapeDtypeStruct((2, size, size), F32),
        ],
        name="prefixes",
    )(inverse_blocks, couplings)


def column_kernel(n_slabs, rows, *refs):
    position, p_ref = refs[0], refs[1]
    arrived = refs[2 : 1 + n_slabs]
    lead_ref = refs[1 + n_slabs]
    green_ref, send_ref, carried = refs[-3:]

    @pl.when(pl.program_id(0) == 0)
    def _():
        carried[...] = lead_ref[0]
        for distance in range(n_slabs - 1, 0, -1):

            @pl.when(position[0] >= distance)
            def _():
                ref = arrived[distance - 1]
                re, im = complex_product(
                    left_parts(ref[0], ref[1]), right_parts(carried[0], carried[1])
                )
                carried[0] = re
                carried[1] = im

    re, im = complex_product(
        left_parts(p_ref[0, 0], p_ref[0, 1]), right_parts(carried[0], carried[1])
    )
    for part, value in enumerate((re, im)):
        green_ref[0, 0, part] = value
        send_ref[:, 0, part] = value.reshape(-1, rows, value.shape[-1])


def columns(position, prefix, arrived, lead, energy, n_energy, green_before):
    blocks, _, size, _ = prefix.shape
    energies = lead.shape[0]
    rows = size // n_energy
    n_slabs = len(arrived) + 1
    whole = pl.BlockSpec((2, size, size), lambda k, s: (0, 0, 0))
    in_specs = [
        pl.BlockSpec((1, 2, size, size), lambda k, s: (k, 0, 0, 0)),
        *[whole] * len(arrived),
        pl.BlockSpec((1, 2, size, size), lambda k, s: (energy, 0, 0, 0)),
    ]
    operands = [prefix, *arrived, lead]
    aliases = {}
    kernel = functools.partial(column_kernel, n_slabs, rows)
    if green_before is not None:
        in_specs.append(pl.BlockSpec(memory_space=pl.ANY))
        operands.append(green_before)
        aliases = {len(operands): 0}
    return pl.pallas_call(
        kernel,
        grid_spec=pltpu.PrefetchScalarGridSpec(
            num_scalar_prefetch=1,
            grid=(blocks,),
            in_specs=in_specs,
            out_specs=[
                pl.BlockSpec((1, 1, 2, size, size), lambda k, s: (energy, k, 0, 0, 0)),
                pl.BlockSpec((n_energy, 1, 2, rows, size), lambda k, s: (0, k, 0, 0, 0)),
            ],
            scratch_shapes=[pltpu.VMEM((2, size, size), F32)],
        ),
        out_shape=[
            jax.ShapeDtypeStruct((energies, blocks, 2, size, size), F32),
            jax.ShapeDtypeStruct((n_energy, blocks, 2, rows, size), F32),
        ],
        input_output_aliases=aliases,
        name="columns",
    )(position, *operands)


def mixing_matrix(energy_index, w_table, local, n_energy):
    grid_points = (w_table.shape[1] + 1) // 2
    order = jnp.arange(n_energy * local).reshape(n_energy, local).T.reshape(-1)
    offsets = energy_index[:, None] - energy_index[order][None, :] + grid_points - 1
    real = w_table[0][offsets]
    imag = w_table[1][offsets]
    pairs = jnp.stack([jnp.stack([real, -imag], -1), jnp.stack([imag, real], -1)], 1)
    spread = pairs[:, :, None, :, :, None] * jnp.eye(SUBLANES, dtype=F32)[:, None, None, :]
    count = energy_index.shape[0] * 2 * SUBLANES
    return spread.reshape(count, count)


def convolve_kernel(*refs):
    mix_ref = refs[0]
    gathered = refs[1:-3]
    out_ref, high, low = refs[-3:]
    rows, lanes = out_ref.shape[-2:]

    @pl.when(pl.program_id(0) == 0)
    def _():
        h, l = split(mix_ref[...])
        high[...] = h
        low[...] = l

    for start in range(0, rows, SUBLANES):
        piece = jnp.concatenate(
            [ref[:, 0, :, start : start + SUBLANES, :].reshape(-1, lanes) for ref in gathered], 0
        )
        mixed = dot3((high[...], low[...]), split(piece))
        out_ref[:, 0, :, start : start + SUBLANES, :] = mixed.reshape(-1, 2, SUBLANES, lanes)


def convolve(mix, gathered):
    n_energy, blocks, _, rows, size = gathered[0].shape
    count = mix.shape[0]
    energies = n_energy * len(gathered)
    return pl.pallas_call(
        convolve_kernel,
        grid=(blocks,),
        in_specs=[
            pl.BlockSpec((count, count), lambda k: (0, 0)),
            *[pl.BlockSpec((n_energy, 1, 2, rows, size), lambda k: (0, k, 0, 0, 0))] * len(gathered),
        ],
        out_specs=pl.BlockSpec((energies, 1, 2, rows, size), lambda k: (0, k, 0, 0, 0)),
        out_shape=jax.ShapeDtypeStruct((energies, blocks, 2, rows, size), F32),
        scratch_shapes=[pltpu.VMEM((count, count), BF16), pltpu.VMEM((count, count), BF16)],
        name="convolve",
    )(mix, *gathered)


def per_device(inverse_blocks, couplings, lead_column, w_table, energy_index):
    n_slabs = lax.axis_size("slab")
    n_energy = lax.axis_size("energy")
    local = inverse_blocks.shape[0]
    position = lax.axis_index("slab").reshape(1).astype(jnp.int32)
    prefix, arrived = [], []
    for energy in range(local):
        p, last = prefixes(inverse_blocks, couplings, energy)
        prefix.append(p)
        arrived.append(
            [
                lax.ppermute(last, "slab", [(i, i + d) for i in range(n_slabs - d)])
                for d in range(1, n_slabs)
            ]
        )
    mix = mixing_matrix(energy_index, w_table, local, n_energy)
    green, gathered = None, []
    for energy in range(local):
        green, send = columns(
            position, prefix[energy], arrived[energy], lead_column, energy, n_energy, green
        )
        gathered.append(lax.all_to_all(send, "energy", 0, 0, tiled=True))
    return green, convolve(mix, gathered)


def solution(mesh):
    placed = (
        P("energy", "slab", None, None, None),
        P("energy", "slab", None, None, None),
        P("energy", None, None, None),
        P(),
        P(),
    )
    return jax.shard_map(
        per_device,
        mesh=mesh,
        in_specs=placed,
        out_specs=(P("energy", "slab", None, None, None), P(None, "slab", None, "energy", None)),
        check_vma=False,
    )
```

profile of v0, /device:TPU:6, one launch (start us, length us, event | category | flops | bytes accessed | tf_op | source)
XLA Modules:
  0.0 179.4 jit_solution(1153009106896298874)
XLA Ops:
  0.6 6.4 %prefixes.3 = (f32[4,2,256,256]{3,2,1,0:T(8,128)}, f32[2,256,256]{2,1,0:T(8,128)}) custom-call(f32[2,4,2,256,256]{4,3,2,1,0:T(8,128)} %g_ref.3, f32[2,4,2,256,256]{4,3,2,1,0:T(8,128)} %h_ref.3), custom_call_target="tpu_custom_call" | custom-call | tf_op jit(solution)/shard_map/prefixes/pallas_call | solution.py:67
  7.0 1.3 collective-permute-start.3
  8.3 1.3 collective-permute-start.4
  9.6 1.3 collective-permute-start.5
  10.9 6.4 %prefixes.2 = (f32[4,2,256,256]{3,2,1,0:T(8,128)}, f32[2,256,256]{2,1,0:T(8,128)}) custom-call(f32[2,4,2,256,256]{4,3,2,1,0:T(8,128)} %g_ref.3, f32[2,4,2,256,256]{4,3,2,1,0:T(8,128)} %h_ref.3), custom_call_target="tpu_custom_call" | custom-call | tf_op jit(solution)/shard_map/prefixes/pallas_call | solution.py:67
  17.2 1.3 collective-permute-start
  18.5 1.3 collective-permute-start.1
  19.8 3.9 %collective-permute-done.3.refs_2_ = f32[2,256,256]{2,1,0:T(8,128)S(1)} collective-permute-done((f32[2,256,256]{2,1,0:T(8,128)}, f32[2,256,256]{2,1,0:T(8,128)S(1)}, u32[]{:S(2)}, u32[]{:S(2)}) %collective-permute-start.3) | collective-permute-done | bytes 524320 | tf_op jit(solution)/shard_map/ppermute | solution.py:211
  23.7 1.3 collective-permute-start.2
  25.0 11.4 %collective-permute-done.4.refs_3_ = f32[2,256,256]{2,1,0:T(8,128)S(1)} collective-permute-done((f32[2,256,256]{2,1,0:T(8,128)}, f32[2,256,256]{2,1,0:T(8,128)S(1)}, u32[]{:S(2)}, u32[]{:S(2)}) %collective-permute-start.4) | collective-permute-done | bytes 524320 | tf_op jit(solution)/shard_map/ppermute | solution.py:211
  36.4 0.8 copy-done.5
  37.2 0.2 copy-done.6
  37.4 7.4 %columns.2 = (f32[2,4,2,256,256]{4,3,2,1,0:T(8,128)}, f32[8,4,2,32,256]{4,3,2,1,0:T(8,128)}) custom-call(s32[1]{0:T(128)} %bitcast.refs_0_, f32[4,2,256,256]{3,2,1,0:T(8,128)} %get-tuple-element.12.refs_1_, f32[2,256,256]{2,1,0:T(8,128)} %copy-done.3, f32[2,256,256]{2,1,0:T(8,128)} %copy-done.5, f32[2,256,256]{2,1,0:T(8,128)} %copy-done.6, ...), custom_call_target="tpu_custom_call" | custom-call | tf_op jit(solution)/shard_map/columns/pallas_call | solution.py:129
  44.8 13.0 %collective-permute-done.1.refs_3_ = f32[2,256,256]{2,1,0:T(8,128)S(1)} collective-permute-done((f32[2,256,256]{2,1,0:T(8,128)}, f32[2,256,256]{2,1,0:T(8,128)S(1)}, u32[]{:S(2)}, u32[]{:S(2)}) %collective-permute-start.1) | collective-permute-done | bytes 524320 | tf_op jit(solution)/shard_map/ppermute | solution.py:211
  57.8 0.8 copy-done.4
  58.5 0.2 copy-done.7
  58.7 7.3 %columns.3 = (f32[2,4,2,256,256]{4,3,2,1,0:T(8,128)}, f32[8,4,2,32,256]{4,3,2,1,0:T(8,128)}) custom-call(s32[1]{0:T(128)} %bitcast.refs_0_, f32[4,2,256,256]{3,2,1,0:T(8,128)} %get-tuple-element.10.refs_1_, f32[2,256,256]{2,1,0:T(8,128)} %copy-done.2, f32[2,256,256]{2,1,0:T(8,128)} %copy-done.4, ...), custom_call_target="tpu_custom_call", output_to_operand_aliasing={{0}: (6, {})} | custom-call | tf_op jit(solution)/shard_map/columns/pallas_call | solution.py:129
  66.1 5.0 %all-to-all-start.1 = ((f32[8,4,2,32,256]{4,3,2,1,0:T(8,128)}), f32[8,4,2,32,256]{4,3,2,1,0:T(8,128)S(1)}, u32[]{:S(2)}, u32[]{:S(2)}) async-start(f32[8,4,2,32,256]{4,3,2,1,0:T(8,128)} %get-tuple-element.17), calls=%async_computation.1 | async-start | bytes 4194304 | tf_op jit(solution)/shard_map/all_to_all | solution.py:221
  71.1 0.1 reshape.130
  71.2 0.7 gather_fusion
  71.9 0.1 reshape.141
  72.0 48.1 %all-to-all-done.1.refs_2_ = f32[8,4,2,32,256]{4,3,2,1,0:T(8,128)S(1)} async-done(((f32[8,4,2,32,256]{4,3,2,1,0:T(8,128)}), f32[8,4,2,32,256]{4,3,2,1,0:T(8,128)S(1)}, u32[]{:S(2)}, u32[]{:S(2)}) %all-to-all-start.1) | async-done | bytes 2097184 | tf_op jit(solution)/shard_map/all_to_all | solution.py:221
  120.1 4.3 %all-to-all-start = ((f32[8,4,2,32,256]{4,3,2,1,0:T(8,128)}), f32[8,4,2,32,256]{4,3,2,1,0:T(8,128)}, u32[]{:S(2)}, u32[]{:S(2)}) async-start(f32[8,4,2,32,256]{4,3,2,1,0:T(8,128)} %get-tuple-element.16), calls=%async_computation | async-start | bytes 4194304 | tf_op jit(solution)/shard_map/all_to_all | solution.py:221
  124.5 0.1 fusion.2
  124.6 1.7 gather_fusion.2
  126.3 0.1 gather.14
  126.4 1.7 gather_fusion.1
  128.2 0.3 copy.9
  128.5 4.2 %broadcast_multiply_fusion = f32[16,2,8,16,2,8]{5,4,3,2,1,0:T(2,128)} fusion(f32[8,8]{1,0:T(8,128)S(1)} %fusion, f32[16,2,16,2]{3,2,1,0:T(8,128)S(1)} %copy.9), kind=kLoop, calls=%fused_computation.3 | loop fusion | flops 65536 | bytes 266496 | tf_op jit(solution)/shard_map/mul | solution.py:157
  132.7 8.5 %mul.20.refs_0_ = f32[256,256]{1,0:T(8,128)} reshape(f32[16,2,8,16,2,8]{5,4,3,2,1,0:T(2,128)} %broadcast_multiply_fusion) | data formatting | bytes 524288 | tf_op jit(solution)/shard_map/mul | solution.py:157
  141.2 32.3 %all-to-all-done.refs_1_ = f32[8,4,2,32,256]{4,3,2,1,0:T(8,128)} async-done(((f32[8,4,2,32,256]{4,3,2,1,0:T(8,128)}), f32[8,4,2,32,256]{4,3,2,1,0:T(8,128)}, u32[]{:S(2)}, u32[]{:S(2)}) %all-to-all-start) | async-done | bytes 2097184 | tf_op jit(solution)/shard_map/all_to_all | solution.py:221
  173.5 5.9 %convolve.1 = f32[16,4,2,32,256]{4,3,2,1,0:T(8,128)} custom-call(f32[256,256]{1,0:T(8,128)} %mul.20.refs_0_, f32[8,4,2,32,256]{4,3,2,1,0:T(8,128)} %all-to-all-done.refs_1_, f32[8,4,2,32,256]{4,3,2,1,0:T(8,128)} %copy-done.1), custom_call_target="tpu_custom_call" | custom-call | tf_op jit(solution)/shard_map/convolve/pallas_call | solution.py:186
  (27 shorter events, 0.2 us)
Async XLA Ops:
  7.0 16.7 %collective-permute-start.3 = (f32[2,256,256]{2,1,0:T(8,128)}, f32[2,256,256]{2,1,0:T(8,128)S(1)}, u32[]{:S(2)}, u32[]{:S(2)}) collective-permute-start(f32[2,256,256]{2,1,0:T(8,128)} %get-tuple-element.13), channel_id=1, source_target_pairs={{0,8},{8,16},{16,24},{1,9},{9,17},{17,25},{2,10},{10,18},{18,26},{... | collective-permute-start | bytes 1572872 | tf_op jit(solution)/shard_map/ppermute | solution.py:211
  8.3 28.1 %collective-permute-start.4 = (f32[2,256,256]{2,1,0:T(8,128)}, f32[2,256,256]{2,1,0:T(8,128)S(1)}, u32[]{:S(2)}, u32[]{:S(2)}) collective-permute-start(f32[2,256,256]{2,1,0:T(8,128)} %get-tuple-element.13), channel_id=1, source_target_pairs={{0,16},{8,24},{1,17},{9,25},{2,18},{10,26},{3,19},{11,27},{4,20},{... | collective-permute-start | bytes 1572872 | tf_op jit(solution)/shard_map/ppermute | solution.py:211
  9.6 26.8 %collective-permute-start.5 = (f32[2,256,256]{2,1,0:T(8,128)}, f32[2,256,256]{2,1,0:T(8,128)S(1)}, u32[]{:S(2)}, u32[]{:S(2)}) collective-permute-start(f32[2,256,256]{2,1,0:T(8,128)} %get-tuple-element.13), channel_id=1, source_target_pairs={{0,24},{1,25},{2,26},{3,27},{4,28},{5,29},{6,30},{7,31}} | collective-permute-start | bytes 1572872 | tf_op jit(solution)/shard_map/ppermute | solution.py:211
  17.2 27.5 %collective-permute-start = (f32[2,256,256]{2,1,0:T(8,128)}, f32[2,256,256]{2,1,0:T(8,128)S(1)}, u32[]{:S(2)}, u32[]{:S(2)}) collective-permute-start(f32[2,256,256]{2,1,0:T(8,128)} %get-tuple-element.11), channel_id=1, source_target_pairs={{0,8},{8,16},{16,24},{1,9},{9,17},{17,25},{2,10},{10,18},{18,26},{... | collective-permute-start | bytes 1572872 | tf_op jit(solution)/shard_map/ppermute | solution.py:211
  18.5 39.2 %collective-permute-start.1 = (f32[2,256,256]{2,1,0:T(8,128)}, f32[2,256,256]{2,1,0:T(8,128)S(1)}, u32[]{:S(2)}, u32[]{:S(2)}) collective-permute-start(f32[2,256,256]{2,1,0:T(8,128)} %get-tuple-element.11), channel_id=1, source_target_pairs={{0,16},{8,24},{1,17},{9,25},{2,18},{10,26},{3,19},{11,27},{4,20},{... | collective-permute-start | bytes 1572872 | tf_op jit(solution)/shard_map/ppermute | solution.py:211
  23.7 12.7 %copy-start.3 = (f32[2,256,256]{2,1,0:T(8,128)}, f32[2,256,256]{2,1,0:T(8,128)S(1)}, u32[]{:S(2)}) copy-start(f32[2,256,256]{2,1,0:T(8,128)S(1)} %collective-permute-done.3.refs_2_) | copy-start | bytes 1572868
  23.7 34.1 %collective-permute-start.2 = (f32[2,256,256]{2,1,0:T(8,128)}, f32[2,256,256]{2,1,0:T(8,128)S(1)}, u32[]{:S(2)}, u32[]{:S(2)}) collective-permute-start(f32[2,256,256]{2,1,0:T(8,128)} %get-tuple-element.11), channel_id=1, source_target_pairs={{0,24},{1,25},{2,26},{3,27},{4,28},{5,29},{6,30},{7,31}} | collective-permute-start | bytes 1572872 | tf_op jit(solution)/shard_map/ppermute | solution.py:211
  36.4 0.8 copy-start.5
  36.4 1.0 copy-start.6
  44.8 13.0 %copy-start.2 = (f32[2,256,256]{2,1,0:T(8,128)}, f32[2,256,256]{2,1,0:T(8,128)S(1)}, u32[]{:S(2)}) copy-start(f32[2,256,256]{2,1,0:T(8,128)S(1)} %collective-permute-done.refs_2_) | copy-start | bytes 1572868
  57.7 0.8 copy-start.4
  57.8 1.0 copy-start.7
  66.1 5.1 %copy-start = (s32[16]{0:T(128)S(1)}, s32[16]{0:T(128)}, u32[]{:S(2)}) copy-start(s32[16]{0:T(128)} %param.9) | copy-start | bytes 196
  66.1 58.4 %copy-start.8 = (f32[2,16383]{1,0:T(2,128)S(1)}, f32[2,16383]{1,0:T(2,128)}, u32[]{:S(2)}) copy-start(f32[2,16383]{1,0:T(2,128)} %param.8) | copy-start | bytes 393196
  66.1 54.0 %all-to-all-start.1 = ((f32[8,4,2,32,256]{4,3,2,1,0:T(8,128)}), f32[8,4,2,32,256]{4,3,2,1,0:T(8,128)S(1)}, u32[]{:S(2)}, u32[]{:S(2)}) async-start(f32[8,4,2,32,256]{4,3,2,1,0:T(8,128)} %get-tuple-element.17), calls=%async_computation.1 | async-start | bytes 4194304 | tf_op jit(solution)/shard_map/all_to_all | solution.py:221
  120.1 6.2 %copy-start.1 = (f32[8,4,2,32,256]{4,3,2,1,0:T(8,128)}, f32[8,4,2,32,256]{4,3,2,1,0:T(8,128)S(1)}, u32[]{:S(2)}) copy-start(f32[8,4,2,32,256]{4,3,2,1,0:T(8,128)S(1)} %all-to-all-done.1.refs_2_) | copy-start | bytes 6291460
  120.1 53.4 %all-to-all-start = ((f32[8,4,2,32,256]{4,3,2,1,0:T(8,128)}), f32[8,4,2,32,256]{4,3,2,1,0:T(8,128)}, u32[]{:S(2)}, u32[]{:S(2)}) async-start(f32[8,4,2,32,256]{4,3,2,1,0:T(8,128)} %get-tuple-element.16), calls=%async_computation | async-start | bytes 4194304 | tf_op jit(solution)/shard_map/all_to_all | solution.py:221
where the time goes:
time: 180 us; the launch traced here: 179 us
  waiting for transfers between devices  109 us (61%)
  Pallas kernels  33.3 us (18%)
  starting transfers between devices  17.1 us (10%)
  local copies, waits for them, and re-layouts  15.2 us (8%)
  other arithmetic  4.34 us (2%)
    all_to_all x2, waiting for transfers between devices, per_device(): gathered.append(lax.all_to_all(send, 'energy', 0, 0, tiled=True))  80.4 us
    ppermute x6, waiting for transfers between devices, per_device(): lax.ppermute(last, 'slab', [(i, i + d) for i in range(n_slabs - d)])  28.3 us
    pallas_call x2, Pallas kernels, columns(): pl.pallas_call(kernel, grid_spec=pltpu.PrefetchScalarGridSpec(num_scalar_...  14.7 us
    pallas_call x2, Pallas kernels, prefixes(): pl.pallas_call(prefix_kernel, grid=(blocks,), in_specs=[spec, spec], out_...  12.7 us
    all_to_all x2, starting transfers between devices, per_device(): gathered.append(lax.all_to_all(send, 'energy', 0, 0, tiled=True))  9.36 us
    mul x1, local copies, waits for them, and re-layouts, mixing_matrix(): pairs[:, :, None, :, :, None]  8.49 us
    ppermute x6, starting transfers between devices, per_device(): lax.ppermute(last, 'slab', [(i, i + d) for i in range(n_slabs - d)])  7.72 us
    pallas_call x1, Pallas kernels, convolve(): pl.pallas_call(convolve_kernel, grid=(blocks,), in_specs=[pl.BlockSpec((c...  5.85 us
  transfers between devices with their start and end apart: 8, of which 5 were waited for; matrix products, arithmetic and copies ran while one was open for 10% of the time, Pallas kernels for 8%

commit v1 on v0

v1 whole, which is shorter than its diff:
```python
import functools

import jax
import jax.numpy as jnp
from jax import lax
from jax.experimental import pallas as pl
from jax.experimental.pallas import tpu as pltpu
from jax.sharding import PartitionSpec as P


F32 = jnp.float32
BF16 = jnp.bfloat16
SUBLANES = 8
LANES = 128
VMEM_LIMIT = 24 * 2**20


def split(x):
    high = x.astype(BF16)
    return high, (x - high.astype(F32)).astype(BF16)


def dot3(left, right):
    def dot(a, b):
        return jnp.dot(a, b, preferred_element_type=F32)

    return dot(left[0], right[0]) + (dot(left[0], right[1]) + dot(left[1], right[0]))


def left_parts(real, imag):
    return split(real + imag), split(real), split(imag)


def right_parts(real, imag):
    return split(real), split(imag - real), split(real + imag)


def complex_product(left, right):
    first = dot3(left[0], right[0])
    second = dot3(left[1], right[1])
    third = dot3(left[2], right[2])
    return first - third, first + second


def compiler_params():
    return pltpu.CompilerParams(vmem_limit_bytes=VMEM_LIMIT)


def prefix_kernel(position, g_ref, h_ref, lead_ref, p_ref, q_ref, *first_refs):
    block = pl.program_id(0)
    real, imag = complex_product(
        left_parts(g_ref[0, 0, 0], g_ref[0, 0, 1]), right_parts(h_ref[0, 0, 0], h_ref[0, 0, 1])
    )
    real, imag = -real, -imag

    @pl.when(block == 0)
    def _():
        q_ref[0] = real
        q_ref[1] = imag

    @pl.when(block > 0)
    def _():
        re, im = complex_product(left_parts(real, imag), right_parts(q_ref[0], q_ref[1]))
        q_ref[0] = re
        q_ref[1] = im

    p_ref[0] = q_ref[...]

    @pl.when((block == pl.num_programs(0) - 1) & (position[0] == 0))
    def _():
        re, im = complex_product(
            left_parts(q_ref[0], q_ref[1]), right_parts(lead_ref[0, 0], lead_ref[0, 1])
        )
        for i, ref in enumerate(first_refs):
            width = ref.shape[-1]
            ref[0] = re[:, i * width : (i + 1) * width]
            ref[1] = im[:, i * width : (i + 1) * width]


def prefixes(position, inverse_blocks, couplings, lead, energy, strips):
    _, blocks, _, size, _ = inverse_blocks.shape
    width = size // strips
    spec = pl.BlockSpec((1, 1, 2, size, size), lambda k, s: (energy, k, 0, 0, 0))
    whole = lambda width: pl.BlockSpec((2, size, width), lambda k, s: (0, 0, 0))
    return pl.pallas_call(
        prefix_kernel,
        grid_spec=pltpu.PrefetchScalarGridSpec(
            num_scalar_prefetch=1,
            grid=(blocks,),
            in_specs=[
                spec,
                spec,
                pl.BlockSpec((1, 2, size, size), lambda k, s: (energy, 0, 0, 0)),
            ],
            out_specs=[
                pl.BlockSpec((1, 2, size, size), lambda k, s: (k, 0, 0, 0)),
                whole(size),
                *[whole(width)] * strips,
            ],
        ),
        out_shape=[
            jax.ShapeDtypeStruct((blocks, 2, size, size), F32),
            jax.ShapeDtypeStruct((2, size, size), F32),
            *[jax.ShapeDtypeStruct((2, size, width), F32)] * strips,
        ],
        compiler_params=compiler_params(),
        name="prefixes",
    )(position, inverse_blocks, couplings, lead)


def column_kernel(n_slabs, n_energy, strip, *refs):
    position, p_ref, lead_ref = refs[:3]
    products = refs[3 : 1 + n_slabs]
    firsts = refs[1 + n_slabs : 2 * n_slabs]
    sends = refs[-1 - n_energy : -1]
    green_ref, carried = refs[-2 - n_energy], refs[-1]
    rows, lanes = sends[0].shape[-2:]

    @pl.when(pl.program_id(0) == 0)
    def _():
        @pl.when(position[0] == 0)
        def _():
            carried[...] = lead_ref[0, :, :, strip * lanes : (strip + 1) * lanes]

        for distance in range(1, n_slabs):

            @pl.when(position[0] == distance)
            def _():
                carried[...] = firsts[distance - 1][...]

        for distance in range(n_slabs - 2, 0, -1):

            @pl.when(position[0] > distance)
            def _():
                ref = products[distance - 1]
                re, im = complex_product(
                    left_parts(ref[0], ref[1]), right_parts(carried[0], carried[1])
                )
                carried[0] = re
                carried[1] = im

    re, im = complex_product(
        left_parts(p_ref[0, 0], p_ref[0, 1]), right_parts(carried[0], carried[1])
    )
    for part, value in enumerate((re, im)):
        green_ref[0, 0, part] = value
    for step, send in enumerate(sends):
        start = pl.multiple_of(partner(position[1], step, n_energy) * rows, rows)
        send[0] = green_ref[0, 0, :, pl.ds(start, rows), :]


def partner(me, step, count):
    if count & (count - 1) == 0:
        return me ^ step
    return (me + step) % count


def columns(position, prefix, lead, products, firsts, energy, strip, n_energy, before):
    blocks, _, size, _ = prefix.shape
    energies = lead.shape[0]
    rows = size // n_energy
    lanes = firsts[0].shape[-1] if firsts else LANES
    n_slabs = len(firsts) + 1
    square = pl.BlockSpec((2, size, size), lambda k, s: (0, 0, 0))
    narrow = pl.BlockSpec((2, size, lanes), lambda k, s: (0, 0, 0))
    in_specs = [
        pl.BlockSpec((1, 2, size, size), lambda k, s: (k, 0, 0, 0)),
        pl.BlockSpec((1, 2, size, size), lambda k, s: (energy, 0, 0, 0)),
        *[square] * len(products),
        *[narrow] * len(firsts),
    ]
    operands = [prefix, lead, *products, *firsts]
    aliases = {}
    if before is not None:
        in_specs.append(pl.BlockSpec(memory_space=pl.ANY))
        operands.append(before)
        aliases = {len(operands): 0}
    green, *sends = pl.pallas_call(
        functools.partial(column_kernel, n_slabs, n_energy, strip),
        grid_spec=pltpu.PrefetchScalarGridSpec(
            num_scalar_prefetch=1,
            grid=(blocks,),
            in_specs=in_specs,
            out_specs=[
                pl.BlockSpec((1, 1, 2, size, lanes), lambda k, s: (energy, k, 0, 0, strip)),
                *[pl.BlockSpec((1, 2, rows, lanes), lambda k, s: (k, 0, 0, 0))] * n_energy,
            ],
            scratch_shapes=[pltpu.VMEM((2, size, lanes), F32)],
        ),
        out_shape=[
            jax.ShapeDtypeStruct((energies, blocks, 2, size, size), F32),
            *[jax.ShapeDtypeStruct((blocks, 2, rows, lanes), F32)] * n_energy,
        ],
        input_output_aliases=aliases,
        compiler_params=compiler_params(),
        name="columns",
    )(position, *operands)
    return green, sends


def spread_kernel(real_ref, imag_ref, high_ref, low_ref):
    energies = real_ref.shape[0]
    count = high_ref.shape[0]
    group = count // energies
    row = lax.broadcasted_iota(jnp.int32, (count, energies), 0) // group
    to_row = (row == lax.broadcasted_iota(jnp.int32, (count, energies), 1)).astype(BF16)
    column = lax.broadcasted_iota(jnp.int32, (energies, count), 1) // group
    to_column = (column == lax.broadcasted_iota(jnp.int32, (energies, count), 0)).astype(BF16)
    rows = lax.broadcasted_iota(jnp.int32, (count, count), 0) % group
    columns = lax.broadcasted_iota(jnp.int32, (count, count), 1) % group
    same_part = rows == columns
    below = rows == columns + SUBLANES
    above = rows + SUBLANES == columns

    def spread(x):
        tall = jnp.dot(to_row, x, preferred_element_type=F32).astype(BF16)
        return jnp.dot(tall, to_column, preferred_element_type=F32)

    for out, real, imag in zip(
        (high_ref, low_ref), split(real_ref[...]), split(imag_ref[...]), strict=True
    ):
        re, im = spread(real), spread(imag)
        out[...] = jnp.where(
            same_part, re, jnp.where(below, im, jnp.where(above, -im, 0.0))
        ).astype(BF16)


def mixing_matrix(energy_index, w_table, local, n_energy):
    grid_points = (w_table.shape[1] + 1) // 2
    energies = energy_index.shape[0]
    sources = partner(lax.axis_index("energy"), jnp.arange(n_energy), n_energy)
    column = energy_index.reshape(n_energy, local)[sources].T.reshape(-1)
    offsets = energy_index[:, None] - column[None, :] + grid_points - 1
    count = energies * 2 * SUBLANES
    return pl.pallas_call(
        spread_kernel,
        out_shape=[jax.ShapeDtypeStruct((count, count), BF16)] * 2,
        compiler_params=compiler_params(),
        name="spread",
    )(w_table[0][offsets], w_table[1][offsets])


def convolve_kernel(count, high_ref, low_ref, *refs):
    gathered, out_ref = refs[:count], refs[-1]
    rows, lanes = out_ref.shape[-2:]
    piece = jnp.concatenate(
        [
            jnp.concatenate(
                [
                    ref[0, :, start : start + SUBLANES, :].reshape(-1, lanes)
                    for start in range(0, rows, SUBLANES)
                ],
                1,
            )
            for ref in gathered
        ],
        0,
    )
    mixed = dot3((high_ref[...], low_ref[...]), split(piece))
    for i, start in enumerate(range(0, rows, SUBLANES)):
        out_ref[:, 0, :, start : start + SUBLANES, :] = mixed[
            :, i * lanes : (i + 1) * lanes
        ].reshape(-1, 2, SUBLANES, lanes)


def convolve(mix, gathered, strip, strips, before):
    blocks, _, rows, lanes = gathered[0].shape
    count = mix[0].shape[0]
    energies = len(gathered)
    matrix = pl.BlockSpec((count, count), lambda k: (0, 0))
    piece = pl.BlockSpec((1, 2, rows, lanes), lambda k: (k, 0, 0, 0))
    in_specs = [matrix, matrix, *[piece] * energies]
    operands = [*mix, *gathered]
    aliases = {}
    if before is not None:
        in_specs.append(pl.BlockSpec(memory_space=pl.ANY))
        operands.append(before)
        aliases = {len(operands) - 1: 0}
    return pl.pallas_call(
        functools.partial(convolve_kernel, energies),
        grid=(blocks,),
        in_specs=in_specs,
        out_specs=pl.BlockSpec((energies, 1, 2, rows, lanes), lambda k: (0, k, 0, 0, strip)),
        out_shape=jax.ShapeDtypeStruct((energies, blocks, 2, rows, strips * lanes), F32),
        input_output_aliases=aliases,
        compiler_params=compiler_params(),
        name="convolve",
    )(*operands)


def per_device(inverse_blocks, couplings, lead_column, w_table, energy_index):
    n_slabs = lax.axis_size("slab")
    n_energy = lax.axis_size("energy")
    local = inverse_blocks.shape[0]
    strips = inverse_blocks.shape[-1] // LANES
    position = jnp.stack([lax.axis_index("slab"), lax.axis_index("energy")]).astype(jnp.int32)
    prefix, products, firsts = [], [], []
    for e in range(local):
        p, last, *first = prefixes(position, inverse_blocks, couplings, lead_column, e, strips)
        prefix.append(p)
        products.append(
            [
                lax.ppermute(last, "slab", [(i, i + d) for i in range(1, n_slabs - d)])
                for d in range(1, n_slabs - 1)
            ]
        )
        firsts.append(
            [[lax.ppermute(one, "slab", [(0, d)]) for d in range(1, n_slabs)] for one in first]
        )
    mix = mixing_matrix(energy_index, w_table, local, n_energy)
    green = None
    gathered = [[None] * (local * n_energy) for _ in range(strips)]
    for e in range(local):
        for strip in range(strips):
            green, sends = columns(
                position,
                prefix[e],
                lead_column,
                products[e],
                firsts[e][strip],
                e,
                strip,
                n_energy,
                green,
            )
            for step in sorted(range(n_energy), reverse=True):
                received = sends[step]
                if step:
                    route = [(i, partner(i, step, n_energy)) for i in range(n_energy)]
                    received = lax.ppermute(received, "energy", route)
                gathered[strip][e * n_energy + step] = received
    mixed = None
    for strip in range(strips):
        mixed = convolve(mix, gathered[strip], strip, strips, mixed)
    return green, mixed


def solution(mesh):
    placed = (
        P("energy", "slab", None, None, None),
        P("energy", "slab", None, None, None),
        P("energy", None, None, None),
        P(),
        P(),
    )
    return jax.shard_map(
        per_device,
        mesh=mesh,
        in_specs=placed,
        out_specs=(P("energy", "slab", None, None, None), P(None, "slab", None, "energy", None)),
        check_vma=False,
    )
```

time: 180 us -> 179 us (level)
  the two profiles are of different devices: /device:TPU:6 before, /device:TPU:17 now
where the time goes in v1:
time: 179 us; the launch traced here: 178 us
  starting transfers between devices  88.6 us (49%)
  waiting for transfers between devices  38.8 us (22%)
  Pallas kernels  30.3 us (17%)
  local copies, waits for them, and re-layouts  19.2 us (11%)
    ppermute x28, starting transfers between devices, per_device(): received = lax.ppermute(received, 'energy', route)  64.1 us
    ppermute x28, waiting for transfers between devices, per_device(): received = lax.ppermute(received, 'energy', route)  24.3 us
    ppermute x12, starting transfers between devices, per_device(): lax.ppermute(one, 'slab', [(0, d)])  21.7 us
    ppermute x12, waiting for transfers between devices, per_device(): lax.ppermute(one, 'slab', [(0, d)])  14.5 us
    pallas_call x4, Pallas kernels, columns(): pl.pallas_call(functools.partial(column_kernel, n_slabs, n_energy, strip)...  14.3 us
    unnamed x32, local copies, waits for them, and re-layouts  12.1 us
    pallas_call x2, Pallas kernels, prefixes(): pl.pallas_call(prefix_kernel, grid_spec=pltpu.PrefetchScalarGridSpec(num_...  9.98 us
    pallas_call x2, Pallas kernels, convolve(): pl.pallas_call(functools.partial(convolve_kernel, energies), grid=(blocks...  5.55 us
  transfers between devices with their start and end apart: 44, of which 16 were waited for; matrix products, arithmetic and copies ran while one was open for 4% of the time, Pallas kernels for 13%

profile of v1, /device:TPU:17, one launch (start us, length us, event | category | flops | bytes accessed | tf_op | source)
XLA Modules:
  0.0 178.0 jit_solution(5783234386967952609)
XLA Ops:
  1.9 2.2 %copy-done.1 = f32[2,4,2,256,256]{4,3,2,1,0:T(8,128)S(1)} copy-done((f32[2,4,2,256,256]{4,3,2,1,0:T(8,128)S(1)}, f32[2,4,2,256,256]{4,3,2,1,0:T(8,128)}, u32[]{:S(2)}) %copy-start.1) | copy-done | bytes 4194328
  4.1 2.2 %copy-done.2 = f32[2,4,2,256,256]{4,3,2,1,0:T(8,128)S(1)} copy-done((f32[2,4,2,256,256]{4,3,2,1,0:T(8,128)S(1)}, f32[2,4,2,256,256]{4,3,2,1,0:T(8,128)}, u32[]{:S(2)}) %copy-start.2) | copy-done | bytes 4194328
  6.3 5.0 %prefixes.3 = (f32[4,2,256,256]{3,2,1,0:T(8,128)S(1)}, f32[2,256,256]{2,1,0:T(8,128)S(1)}, f32[2,256,128]{2,1,0:T(8,128)S(1)}, f32[2,256,128]{2,1,0:T(8,128)S(1)}) custom-call(s32[2]{0:T(128)S(1)} %pad_add_fusion.position.refs_0_, f32[2,4,2,256,256]{4,3,2,1,0:T(8,128)S(1)} %copy-done.1, f32[2,4,2,256,256]{4,3,2,1,0:T(8,128)S(1)} %copy-done.2, ...), custom_call_target="tpu_custom_call" | custom-call | tf_op jit(solution)/shard_map/prefixes/pallas_call | solution.py:85
  11.3 2.6 %collective-permute-start.13 = (f32[2,256,128]{2,1,0:T(8,128)S(1)}, f32[2,256,128]{2,1,0:T(8,128)S(1)}, u32[]{:S(2)}, u32[]{:S(2)}) collective-permute-start(f32[2,256,128]{2,1,0:T(8,128)S(1)} %get-tuple-element.55), channel_id=1, source_target_pairs={{0,8},{1,9},{2,10},{3,11},{4,12},{5,13},{6,14},{7,15}} | collective-permute-start | bytes 786440 | tf_op jit(solution)/shard_map/ppermute | solution.py:308
  19.2 5.0 %prefixes.2 = (f32[4,2,256,256]{3,2,1,0:T(8,128)S(1)}, f32[2,256,256]{2,1,0:T(8,128)S(1)}, f32[2,256,128]{2,1,0:T(8,128)S(1)}, f32[2,256,128]{2,1,0:T(8,128)S(1)}) custom-call(s32[2]{0:T(128)S(1)} %pad_add_fusion.position.refs_0_, f32[2,4,2,256,256]{4,3,2,1,0:T(8,128)S(1)} %copy-done.1, f32[2,4,2,256,256]{4,3,2,1,0:T(8,128)S(1)} %copy-done.2, ...), custom_call_target="tpu_custom_call" | custom-call | tf_op jit(solution)/shard_map/prefixes/pallas_call | solution.py:85
  31.5 4.2 %collective-permute-done.12.refs_7_ = f32[2,256,128]{2,1,0:T(8,128)S(1)} collective-permute-done((f32[2,256,128]{2,1,0:T(8,128)S(1)}, f32[2,256,128]{2,1,0:T(8,128)S(1)}, u32[]{:S(2)}, u32[]{:S(2)}) %collective-permute-start.12) | collective-permute-done | bytes 262176 | tf_op jit(solution)/shard_map/ppermute | solution.py:308
  36.4 4.9 %collective-permute-done.5.refs_5_ = f32[2,256,128]{2,1,0:T(8,128)S(1)} collective-permute-done((f32[2,256,128]{2,1,0:T(8,128)S(1)}, f32[2,256,128]{2,1,0:T(8,128)S(1)}, u32[]{:S(2)}, u32[]{:S(2)}) %collective-permute-start.5) | collective-permute-done | bytes 262176 | tf_op jit(solution)/shard_map/ppermute | solution.py:308
  43.4 3.3 %collective-permute-done.7.refs_7_ = f32[2,256,128]{2,1,0:T(8,128)S(1)} collective-permute-done((f32[2,256,128]{2,1,0:T(8,128)S(1)}, f32[2,256,128]{2,1,0:T(8,128)S(1)}, u32[]{:S(2)}, u32[]{:S(2)}) %collective-permute-start.7) | collective-permute-done | bytes 262176 | tf_op jit(solution)/shard_map/ppermute | solution.py:308
  49.3 6.1 %collective-permute-start.4 = (f32[2,256,128]{2,1,0:T(8,128)S(1)}, f32[2,256,128]{2,1,0:T(8,128)S(1)}, u32[]{:S(2)}, u32[]{:S(2)}) collective-permute-start(f32[2,256,128]{2,1,0:T(8,128)S(1)} %get-tuple-element.50), channel_id=1, source_target_pairs={{0,24},{1,25},{2,26},{3,27},{4,28},{5,29},{6,30},{7,31}} | collective-permute-start | bytes 786440 | tf_op jit(solution)/shard_map/ppermute | solution.py:308
  55.4 3.6 %columns.4 = (f32[2,4,2,256,256]{4,3,2,1,0:T(8,128)}, f32[4,2,32,128]{3,2,1,0:T(8,128)S(1)}, f32[4,2,32,128]{3,2,1,0:T(8,128)S(1)}, f32[4,2,32,128]{3,2,1,0:T(8,...) custom-call(s32[2]{0:T(128)S(1)} %pad_add_fusion.position.refs_0_, ...), custom_call_target="tpu_custom_call" | custom-call | tf_op jit(solution)/shard_map/columns/pallas_call | solution.py:178
  59.0 3.6 %columns.5 = (f32[2,4,2,256,256]{4,3,2,1,0:T(8,128)}, f32[4,2,32,128]{3,2,1,0:T(8,128)S(1)}, f32[4,2,32,128]{3,2,1,0:T(8,128)S(1)}, f32[4,2,32,128]{3,2,1,0:T(8,...) custom-call(s32[2]{0:T(128)S(1)} %pad_add_fusion.position.refs_0_, ...), custom_call_target="tpu_custom_call", output_to_operand_aliasing={{0}: (8, {})} | custom-call | tf_op jit(solution)/shard_map/columns/pallas_call | solution.py:178
  62.6 3.6 %columns.6 = (f32[2,4,2,256,256]{4,3,2,1,0:T(8,128)}, f32[4,2,32,128]{3,2,1,0:T(8,128)S(1)}, f32[4,2,32,128]{3,2,1,0:T(8,128)S(1)}, f32[4,2,32,128]{3,2,1,0:T(8,...) custom-call(s32[2]{0:T(128)S(1)} %pad_add_fusion.position.refs_0_, ...), custom_call_target="tpu_custom_call", output_to_operand_aliasing={{0}: (8, {})} | custom-call | tf_op jit(solution)/shard_map/columns/pallas_call | solution.py:178
  66.2 14.0 %collective-permute-start.37 = (f32[4,2,32,128]{3,2,1,0:T(8,128)S(1)}, f32[4,2,32,128]{3,2,1,0:T(8,128)S(1)}, u32[]{:S(2)}, u32[]{:S(2)}) collective-permute-start(f32[4,2,32,128]{3,2,1,0:T(8,128)S(1)} %get-tuple-element.87), channel_id=1, source_target_pairs={{0,1},{1,0},{2,3},{3,2},{4,5},{5,4},{6,7},{7,6},{8,9},{9,8},{10,11... | collective-permute-start | bytes 393224 | tf_op jit(solution)/shard_map/ppermute | solution.py:330
  81.8 2.7 %collective-permute-start.41 = (f32[4,2,32,128]{3,2,1,0:T(8,128)S(1)}, f32[4,2,32,128]{3,2,1,0:T(8,128)S(1)}, u32[]{:S(2)}, u32[]{:S(2)}) collective-permute-start(f32[4,2,32,128]{3,2,1,0:T(8,128)S(1)} %get-tuple-element.91), channel_id=1, source_target_pairs={{0,5},{1,4},{2,7},{3,6},{4,1},{5,0},{6,3},{7,2},{8,13},{9,12},{10,... | collective-permute-start | bytes 393224 | tf_op jit(solution)/shard_map/ppermute | solution.py:330
  85.2 4.1 %collective-permute-start.43 = (f32[4,2,32,128]{3,2,1,0:T(8,128)S(1)}, f32[4,2,32,128]{3,2,1,0:T(8,128)S(1)}, u32[]{:S(2)}, u32[]{:S(2)}) collective-permute-start(f32[4,2,32,128]{3,2,1,0:T(8,128)S(1)} %get-tuple-element.93), channel_id=1, source_target_pairs={{0,7},{1,6},{2,5},{3,4},{4,3},{5,2},{6,1},{7,0},{8,15},{9,14},{10,... | collective-permute-start | bytes 393224 | tf_op jit(solution)/shard_map/ppermute | solution.py:330
  90.9 2.0 %collective-permute-start.31 = (f32[4,2,32,128]{3,2,1,0:T(8,128)S(1)}, f32[4,2,32,128]{3,2,1,0:T(8,128)S(1)}, u32[]{:S(2)}, u32[]{:S(2)}) collective-permute-start(f32[4,2,32,128]{3,2,1,0:T(8,128)S(1)} %get-tuple-element.80), channel_id=1, source_target_pairs={{0,2},{1,3},{2,0},{3,1},{4,6},{5,7},{6,4},{7,5},{8,10},{9,11},{10,... | collective-permute-start | bytes 393224 | tf_op jit(solution)/shard_map/ppermute | solution.py:330
  94.2 9.0 %collective-permute-start.32 = (f32[4,2,32,128]{3,2,1,0:T(8,128)S(1)}, f32[4,2,32,128]{3,2,1,0:T(8,128)S(1)}, u32[]{:S(2)}, u32[]{:S(2)}) collective-permute-start(f32[4,2,32,128]{3,2,1,0:T(8,128)S(1)} %get-tuple-element.81), channel_id=1, source_target_pairs={{0,3},{1,2},{2,1},{3,0},{4,7},{5,6},{6,5},{7,4},{8,11},{9,10},{10,... | collective-permute-start | bytes 393224 | tf_op jit(solution)/shard_map/ppermute | solution.py:330
  104.6 5.3 %collective-permute-done.43.refs_15_ = f32[4,2,32,128]{3,2,1,0:T(8,128)S(1)} collective-permute-done((f32[4,2,32,128]{3,2,1,0:T(8,128)S(1)}, f32[4,2,32,128]{3,2,1,0:T(8,128)S(1)}, u32[]{:S(2)}, u32[]{:S(2)}) %collective-permute-start.43) | collective-permute-done | bytes 131104 | tf_op jit(solution)/shard_map/ppermute | solution.py:330
  109.9 3.6 %columns.7 = (f32[2,4,2,256,256]{4,3,2,1,0:T(8,128)}, f32[4,2,32,128]{3,2,1,0:T(8,128)S(1)}, f32[4,2,32,128]{3,2,1,0:T(8,128)S(1)}, f32[4,2,32,128]{3,2,1,0:T(8,...) custom-call(s32[2]{0:T(128)S(1)} %pad_add_fusion.position.refs_0_, ...), custom_call_target="tpu_custom_call", output_to_operand_aliasing={{0}: (8, {})} | custom-call | tf_op jit(solution)/shard_map/columns/pallas_call | solution.py:178
  115.3 4.5 %collective-permute-start.24 = (f32[4,2,32,128]{3,2,1,0:T(8,128)S(1)}, f32[4,2,32,128]{3,2,1,0:T(8,128)S(1)}, u32[]{:S(2)}, u32[]{:S(2)}) collective-permute-start(f32[4,2,32,128]{3,2,1,0:T(8,128)S(1)} %get-tuple-element.72), channel_id=1, source_target_pairs={{0,2},{1,3},{2,0},{3,1},{4,6},{5,7},{6,4},{7,5},{8,10},{9,11},{10,... | collective-permute-start | bytes 393224 | tf_op jit(solution)/shard_map/ppermute | solution.py:330
  121.1 5.3 %collective-permute-start.25 = (f32[4,2,32,128]{3,2,1,0:T(8,128)S(1)}, f32[4,2,32,128]{3,2,1,0:T(8,128)S(1)}, u32[]{:S(2)}, u32[]{:S(2)}) collective-permute-start(f32[4,2,32,128]{3,2,1,0:T(8,128)S(1)} %get-tuple-element.73), channel_id=1, source_target_pairs={{0,3},{1,2},{2,1},{3,0},{4,7},{5,6},{6,5},{7,4},{8,11},{9,10},{10,... | collective-permute-start | bytes 393224 | tf_op jit(solution)/shard_map/ppermute | solution.py:330
  128.5 2.3 %collective-permute-done.36.refs_7_ = f32[4,2,32,128]{3,2,1,0:T(8,128)S(1)} collective-permute-done((f32[4,2,32,128]{3,2,1,0:T(8,128)S(1)}, f32[4,2,32,128]{3,2,1,0:T(8,128)S(1)}, u32[]{:S(2)}, u32[]{:S(2)}) %collective-permute-start.36) | collective-permute-done | bytes 131104 | tf_op jit(solution)/shard_map/ppermute | solution.py:330
  131.4 2.0 %collective-permute-start.27 = (f32[4,2,32,128]{3,2,1,0:T(8,128)S(1)}, f32[4,2,32,128]{3,2,1,0:T(8,128)S(1)}, u32[]{:S(2)}, u32[]{:S(2)}) collective-permute-start(f32[4,2,32,128]{3,2,1,0:T(8,128)S(1)} %get-tuple-element.75), channel_id=1, source_target_pairs={{0,5},{1,4},{2,7},{3,6},{4,1},{5,0},{6,3},{7,2},{8,13},{9,12},{10,... | collective-permute-start | bytes 393224 | tf_op jit(solution)/shard_map/ppermute | solution.py:330
  135.3 10.2 %collective-permute-start.17 = (f32[4,2,32,128]{3,2,1,0:T(8,128)S(1)}, f32[4,2,32,128]{3,2,1,0:T(8,128)S(1)}, u32[]{:S(2)}, u32[]{:S(2)}) collective-permute-start(f32[4,2,32,128]{3,2,1,0:T(8,128)S(1)} %get-tuple-element.64), channel_id=1, source_target_pairs={{0,2},{1,3},{2,0},{3,1},{4,6},{5,7},{6,4},{7,5},{8,10},{9,11},{10,... | collective-permute-start | bytes 393224 | tf_op jit(solution)/shard_map/ppermute | solution.py:330
  146.3 2.3 %collective-permute-start.18 = (f32[4,2,32,128]{3,2,1,0:T(8,128)}, f32[4,2,32,128]{3,2,1,0:T(8,128)S(1)}, u32[]{:S(2)}, u32[]{:S(2)}) collective-permute-start(f32[4,2,32,128]{3,2,1,0:T(8,128)} %get-tuple-element.65), channel_id=1, source_target_pairs={{0,3},{1,2},{2,1},{3,0},{4,7},{5,6},{6,5},{7,4},{8,11},{9,10},{10,... | collective-permute-start | bytes 393224 | tf_op jit(solution)/shard_map/ppermute | solution.py:330
  149.9 3.2 %collective-permute-done.29.refs_15_ = f32[4,2,32,128]{3,2,1,0:T(8,128)S(1)} collective-permute-done((f32[4,2,32,128]{3,2,1,0:T(8,128)S(1)}, f32[4,2,32,128]{3,2,1,0:T(8,128)S(1)}, u32[]{:S(2)}, u32[]{:S(2)}) %collective-permute-start.29) | collective-permute-done | bytes 131104 | tf_op jit(solution)/shard_map/ppermute | solution.py:330
  154.9 2.1 %gather_fusion.2 = f32[256]{0:T(256)S(1)} fusion(f32[16383]{0:T(1024)} %bitcast.10, s32[1024]{0:T(1024)S(1)} %pad_clamp_fusion), kind=kCustom, calls=%fused_computation.2 | custom fusion | bytes 3072 | tf_op jit(solution)/shard_map/gather | solution.py:240
  157.1 2.6 %gather_fusion.1 = f32[256]{0:T(256)} fusion(f32[16383]{0:T(1024)} %bitcast.9, s32[1024]{0:T(1024)S(1)} %pad_clamp_fusion), kind=kCustom, calls=%fused_computation.1 | custom fusion | bytes 3072 | tf_op jit(solution)/shard_map/gather | solution.py:240
  165.4 2.8 %convolve.2.refs_16_ = f32[16,4,2,32,256]{4,3,2,1,0:T(8,128)} custom-call(bf16[256,256]{1,0:T(8,128)(2,1)S(1)} %get-tuple-element.60.high_ref, bf16[256,256]{1,0:T(8,128)(2,1)S(1)} %get-tuple-element.61.low_ref, f32[4,2,32,128]{3,2,1,0:T(8,128)S(1)} %get-tuple-element.78.refs_0_, f32[4,2,32,128]{3,2,1,0:T(8,128)S(1)} %collective-permute-done.30.refs_1_, ...), custom_call_target="tpu_custom_call" | custom-call | tf_op jit(solution)/shard_map/convolve/pallas_call | solution.py:279
  168.2 4.0 %collective-permute-done.21.refs_6_ = f32[4,2,32,128]{3,2,1,0:T(8,128)S(1)} collective-permute-done((f32[4,2,32,128]{3,2,1,0:T(8,128)}, f32[4,2,32,128]{3,2,1,0:T(8,128)S(1)}, u32[]{:S(2)}, u32[]{:S(2)}) %collective-permute-start.21) | collective-permute-done | bytes 131104 | tf_op jit(solution)/shard_map/ppermute | solution.py:330
  172.2 3.0 %collective-permute-done.22.refs_7_ = f32[4,2,32,128]{3,2,1,0:T(8,128)S(1)} collective-permute-done((f32[4,2,32,128]{3,2,1,0:T(8,128)}, f32[4,2,32,128]{3,2,1,0:T(8,128)S(1)}, u32[]{:S(2)}, u32[]{:S(2)}) %collective-permute-start.22) | collective-permute-done | bytes 131104 | tf_op jit(solution)/shard_map/ppermute | solution.py:330
  175.2 2.8 %convolve.3 = f32[16,4,2,32,256]{4,3,2,1,0:T(8,128)} custom-call(bf16[256,256]{1,0:T(8,128)(2,1)S(1)} %get-tuple-element.60.high_ref, bf16[256,256]{1,0:T(8,128)(2,1)S(1)} %get-tuple-element.61.low_ref, f32[4,2,32,128]{3,2,1,0:T(8,128)S(1)} %get-tuple-element.62.refs_0_, ...), custom_call_target="tpu_custom_call", output_to_operand_aliasing={{}: (18, {})} | custom-call | tf_op jit(solution)/shard_map/convolve/pallas_call | solution.py:279
  (112 shorter events, 43.1 us)
Async XLA Ops:
  11.3 12.8 %collective-permute-start.13 = (f32[2,256,128]{2,1,0:T(8,128)S(1)}, f32[2,256,128]{2,1,0:T(8,128)S(1)}, u32[]{:S(2)}, u32[]{:S(2)}) collective-permute-start(f32[2,256,128]{2,1,0:T(8,128)S(1)} %get-tuple-element.55), channel_id=1, source_target_pairs={{0,8},{1,9},{2,10},{3,11},{4,12},{5,13},{6,14},{7,15}} | collective-permute-start | bytes 786440 | tf_op jit(solution)/shard_map/ppermute | solution.py:308
  16.5 13.6 %collective-permute-start.10 = (f32[2,256,128]{2,1,0:T(8,128)S(1)}, f32[2,256,128]{2,1,0:T(8,128)S(1)}, u32[]{:S(2)}, u32[]{:S(2)}) collective-permute-start(f32[2,256,128]{2,1,0:T(8,128)S(1)} %get-tuple-element.54), channel_id=1, source_target_pairs={{0,8},{1,9},{2,10},{3,11},{4,12},{5,13},{6,14},{7,15}} | collective-permute-start | bytes 786440 | tf_op jit(solution)/shard_map/ppermute | solution.py:308
  17.9 12.9 %collective-permute-start.11 = (f32[2,256,128]{2,1,0:T(8,128)S(1)}, f32[2,256,128]{2,1,0:T(8,128)S(1)}, u32[]{:S(2)}, u32[]{:S(2)}) collective-permute-start(f32[2,256,128]{2,1,0:T(8,128)S(1)} %get-tuple-element.54), channel_id=1, source_target_pairs={{0,16},{1,17},{2,18},{3,19},{4,20},{5,21},{6,22},{7,23}} | collective-permute-start | bytes 786440 | tf_op jit(solution)/shard_map/ppermute | solution.py:308
  25.5 15.8 %collective-permute-start.5 = (f32[2,256,128]{2,1,0:T(8,128)S(1)}, f32[2,256,128]{2,1,0:T(8,128)S(1)}, u32[]{:S(2)}, u32[]{:S(2)}) collective-permute-start(f32[2,256,128]{2,1,0:T(8,128)S(1)} %get-tuple-element.51), channel_id=1, source_target_pairs={{0,8},{1,9},{2,10},{3,11},{4,12},{5,13},{6,14},{7,15}} | collective-permute-start | bytes 786440 | tf_op jit(solution)/shard_map/ppermute | solution.py:308
  26.8 15.2 %collective-permute-start.6 = (f32[2,256,128]{2,1,0:T(8,128)S(1)}, f32[2,256,128]{2,1,0:T(8,128)S(1)}, u32[]{:S(2)}, u32[]{:S(2)}) collective-permute-start(f32[2,256,128]{2,1,0:T(8,128)S(1)} %get-tuple-element.51), channel_id=1, source_target_pairs={{0,16},{1,17},{2,18},{3,19},{4,20},{5,21},{6,22},{7,23}} | collective-permute-start | bytes 786440 | tf_op jit(solution)/shard_map/ppermute | solution.py:308
  30.1 17.9 %collective-permute-start.8 = (f32[2,256,256]{2,1,0:T(8,128)S(1)}, f32[2,256,256]{2,1,0:T(8,128)S(1)}, u32[]{:S(2)}, u32[]{:S(2)}) collective-permute-start(f32[2,256,256]{2,1,0:T(8,128)S(1)} %get-tuple-element.53), channel_id=1, source_target_pairs={{8,16},{16,24},{9,17},{17,25},{10,18},{18,26},{11,19},{19,27},{12,... | collective-permute-start | bytes 1572872 | tf_op jit(solution)/shard_map/ppermute | solution.py:303
  30.8 18.5 %collective-permute-start.9 = (f32[2,256,256]{2,1,0:T(8,128)S(1)}, f32[2,256,256]{2,1,0:T(8,128)S(1)}, u32[]{:S(2)}, u32[]{:S(2)}) collective-permute-start(f32[2,256,256]{2,1,0:T(8,128)S(1)} %get-tuple-element.53), channel_id=1, source_target_pairs={{8,24},{9,25},{10,26},{11,27},{12,28},{13,29},{14,30},{15,31}} | collective-permute-start | bytes 1572872 | tf_op jit(solution)/shard_map/ppermute | solution.py:303
  35.7 26.9 %collective-permute-start = (f32[2,256,256]{2,1,0:T(8,128)S(1)}, f32[2,256,256]{2,1,0:T(8,128)S(1)}, u32[]{:S(2)}, u32[]{:S(2)}) collective-permute-start(f32[2,256,256]{2,1,0:T(8,128)S(1)} %get-tuple-element.49), channel_id=1, source_target_pairs={{8,16},{16,24},{9,17},{17,25},{10,18},{18,26},{11,19},{19,27},{12,... | collective-permute-start | bytes 1572872 | tf_op jit(solution)/shard_map/ppermute | solution.py:303
  41.3 21.2 %collective-permute-start.1 = (f32[2,256,256]{2,1,0:T(8,128)S(1)}, f32[2,256,256]{2,1,0:T(8,128)S(1)}, u32[]{:S(2)}, u32[]{:S(2)}) collective-permute-start(f32[2,256,256]{2,1,0:T(8,128)S(1)} %get-tuple-element.49), channel_id=1, source_target_pairs={{8,24},{9,25},{10,26},{11,27},{12,28},{13,29},{14,30},{15,31}} | collective-permute-start | bytes 1572872 | tf_op jit(solution)/shard_map/ppermute | solution.py:303
  46.7 34.7 %collective-permute-start.2 = (f32[2,256,128]{2,1,0:T(8,128)S(1)}, f32[2,256,128]{2,1,0:T(8,128)S(1)}, u32[]{:S(2)}, u32[]{:S(2)}) collective-permute-start(f32[2,256,128]{2,1,0:T(8,128)S(1)} %get-tuple-element.50), channel_id=1, source_target_pairs={{0,8},{1,9},{2,10},{3,11},{4,12},{5,13},{6,14},{7,15}} | collective-permute-start | bytes 786440 | tf_op jit(solution)/shard_map/ppermute | solution.py:308
  48.0 33.8 %collective-permute-start.3 = (f32[2,256,128]{2,1,0:T(8,128)S(1)}, f32[2,256,128]{2,1,0:T(8,128)S(1)}, u32[]{:S(2)}, u32[]{:S(2)}) collective-permute-start(f32[2,256,128]{2,1,0:T(8,128)S(1)} %get-tuple-element.50), channel_id=1, source_target_pairs={{0,16},{1,17},{2,18},{3,19},{4,20},{5,21},{6,22},{7,23}} | collective-permute-start | bytes 786440 | tf_op jit(solution)/shard_map/ppermute | solution.py:308
  49.3 32.5 %collective-permute-start.4 = (f32[2,256,128]{2,1,0:T(8,128)S(1)}, f32[2,256,128]{2,1,0:T(8,128)S(1)}, u32[]{:S(2)}, u32[]{:S(2)}) collective-permute-start(f32[2,256,128]{2,1,0:T(8,128)S(1)} %get-tuple-element.50), channel_id=1, source_target_pairs={{0,24},{1,25},{2,26},{3,27},{4,28},{5,29},{6,30},{7,31}} | collective-permute-start | bytes 786440 | tf_op jit(solution)/shard_map/ppermute | solution.py:308
  66.2 18.4 %collective-permute-start.37 = (f32[4,2,32,128]{3,2,1,0:T(8,128)S(1)}, f32[4,2,32,128]{3,2,1,0:T(8,128)S(1)}, u32[]{:S(2)}, u32[]{:S(2)}) collective-permute-start(f32[4,2,32,128]{3,2,1,0:T(8,128)S(1)} %get-tuple-element.87), channel_id=1, source_target_pairs={{0,1},{1,0},{2,3},{3,2},{4,5},{5,4},{6,7},{7,6},{8,9},{9,8},{10,11... | collective-permute-start | bytes 393224 | tf_op jit(solution)/shard_map/ppermute | solution.py:330
  84.5 20.0 %collective-permute-start.42 = (f32[4,2,32,128]{3,2,1,0:T(8,128)S(1)}, f32[4,2,32,128]{3,2,1,0:T(8,128)S(1)}, u32[]{:S(2)}, u32[]{:S(2)}) collective-permute-start(f32[4,2,32,128]{3,2,1,0:T(8,128)S(1)} %get-tuple-element.92), channel_id=1, source_target_pairs={{0,6},{1,7},{2,4},{3,5},{4,2},{5,3},{6,0},{7,1},{8,14},{9,15},{10,... | collective-permute-start | bytes 393224 | tf_op jit(solution)/shard_map/ppermute | solution.py:330
  85.2 24.7 %collective-permute-start.43 = (f32[4,2,32,128]{3,2,1,0:T(8,128)S(1)}, f32[4,2,32,128]{3,2,1,0:T(8,128)S(1)}, u32[]{:S(2)}, u32[]{:S(2)}) collective-permute-start(f32[4,2,32,128]{3,2,1,0:T(8,128)S(1)} %get-tuple-element.93), channel_id=1, source_target_pairs={{0,7},{1,6},{2,5},{3,4},{4,3},{5,2},{6,1},{7,0},{8,15},{9,14},{10,... | collective-permute-start | bytes 393224 | tf_op jit(solution)/shard_map/ppermute | solution.py:330
  90.0 19.9 %collective-permute-start.30 = (f32[4,2,32,128]{3,2,1,0:T(8,128)S(1)}, f32[4,2,32,128]{3,2,1,0:T(8,128)S(1)}, u32[]{:S(2)}, u32[]{:S(2)}) collective-permute-start(f32[4,2,32,128]{3,2,1,0:T(8,128)S(1)} %get-tuple-element.79), channel_id=1, source_target_pairs={{0,1},{1,0},{2,3},{3,2},{4,5},{5,4},{6,7},{7,6},{8,9},{9,8},{10,11... | collective-permute-start | bytes 393224 | tf_op jit(solution)/shard_map/ppermute | solution.py:330
  90.9 22.6 %collective-permute-start.31 = (f32[4,2,32,128]{3,2,1,0:T(8,128)S(1)}, f32[4,2,32,128]{3,2,1,0:T(8,128)S(1)}, u32[]{:S(2)}, u32[]{:S(2)}) collective-permute-start(f32[4,2,32,128]{3,2,1,0:T(8,128)S(1)} %get-tuple-element.80), channel_id=1, source_target_pairs={{0,2},{1,3},{2,0},{3,1},{4,6},{5,7},{6,4},{7,5},{8,10},{9,11},{10,... | collective-permute-start | bytes 393224 | tf_op jit(solution)/shard_map/ppermute | solution.py:330
  94.2 19.2 %collective-permute-start.32 = (f32[4,2,32,128]{3,2,1,0:T(8,128)S(1)}, f32[4,2,32,128]{3,2,1,0:T(8,128)S(1)}, u32[]{:S(2)}, u32[]{:S(2)}) collective-permute-start(f32[4,2,32,128]{3,2,1,0:T(8,128)S(1)} %get-tuple-element.81), channel_id=1, source_target_pairs={{0,3},{1,2},{2,1},{3,0},{4,7},{5,6},{6,5},{7,4},{8,11},{9,10},{10,... | collective-permute-start | bytes 393224 | tf_op jit(solution)/shard_map/ppermute | solution.py:330
  109.9 17.2 %collective-permute-start.35 = (f32[4,2,32,128]{3,2,1,0:T(8,128)S(1)}, f32[4,2,32,128]{3,2,1,0:T(8,128)S(1)}, u32[]{:S(2)}, u32[]{:S(2)}) collective-permute-start(f32[4,2,32,128]{3,2,1,0:T(8,128)S(1)} %get-tuple-element.84), channel_id=1, source_target_pairs={{0,6},{1,7},{2,4},{3,5},{4,2},{5,3},{6,0},{7,1},{8,14},{9,15},{10,... | collective-permute-start | bytes 393224 | tf_op jit(solution)/shard_map/ppermute | solution.py:330
  113.5 17.3 %collective-permute-start.36 = (f32[4,2,32,128]{3,2,1,0:T(8,128)S(1)}, f32[4,2,32,128]{3,2,1,0:T(8,128)S(1)}, u32[]{:S(2)}, u32[]{:S(2)}) collective-permute-start(f32[4,2,32,128]{3,2,1,0:T(8,128)S(1)} %get-tuple-element.85), channel_id=1, source_target_pairs={{0,7},{1,6},{2,5},{3,4},{4,3},{5,2},{6,1},{7,0},{8,15},{9,14},{10,... | collective-permute-start | bytes 393224 | tf_op jit(solution)/shard_map/ppermute | solution.py:330
  113.5 20.0 %collective-permute-start.23 = (f32[4,2,32,128]{3,2,1,0:T(8,128)S(1)}, f32[4,2,32,128]{3,2,1,0:T(8,128)S(1)}, u32[]{:S(2)}, u32[]{:S(2)}) collective-permute-start(f32[4,2,32,128]{3,2,1,0:T(8,128)S(1)} %get-tuple-element.71), channel_id=1, source_target_pairs={{0,1},{1,0},{2,3},{3,2},{4,5},{5,4},{6,7},{7,6},{8,9},{9,8},{10,11... | collective-permute-start | bytes 393224 | tf_op jit(solution)/shard_map/ppermute | solution.py:330
  115.3 18.2 %collective-permute-start.24 = (f32[4,2,32,128]{3,2,1,0:T(8,128)S(1)}, f32[4,2,32,128]{3,2,1,0:T(8,128)S(1)}, u32[]{:S(2)}, u32[]{:S(2)}) collective-permute-start(f32[4,2,32,128]{3,2,1,0:T(8,128)S(1)} %get-tuple-element.72), channel_id=1, source_target_pairs={{0,2},{1,3},{2,0},{3,1},{4,6},{5,7},{6,4},{7,5},{8,10},{9,11},{10,... | collective-permute-start | bytes 393224 | tf_op jit(solution)/shard_map/ppermute | solution.py:330
  131.4 14.9 %collective-permute-start.27 = (f32[4,2,32,128]{3,2,1,0:T(8,128)S(1)}, f32[4,2,32,128]{3,2,1,0:T(8,128)S(1)}, u32[]{:S(2)}, u32[]{:S(2)}) collective-permute-start(f32[4,2,32,128]{3,2,1,0:T(8,128)S(1)} %get-tuple-element.75), channel_id=1, source_target_pairs={{0,5},{1,4},{2,7},{3,6},{4,1},{5,0},{6,3},{7,2},{8,13},{9,12},{10,... | collective-permute-start | bytes 393224 | tf_op jit(solution)/shard_map/ppermute | solution.py:330
  133.4 16.5 %collective-permute-start.28 = (f32[4,2,32,128]{3,2,1,0:T(8,128)S(1)}, f32[4,2,32,128]{3,2,1,0:T(8,128)S(1)}, u32[]{:S(2)}, u32[]{:S(2)}) collective-permute-start(f32[4,2,32,128]{3,2,1,0:T(8,128)S(1)} %get-tuple-element.76), channel_id=1, source_target_pairs={{0,6},{1,7},{2,4},{3,5},{4,2},{5,3},{6,0},{7,1},{8,14},{9,15},{10,... | collective-permute-start | bytes 393224 | tf_op jit(solution)/shard_map/ppermute | solution.py:330
  133.5 19.7 %collective-permute-start.29 = (f32[4,2,32,128]{3,2,1,0:T(8,128)S(1)}, f32[4,2,32,128]{3,2,1,0:T(8,128)S(1)}, u32[]{:S(2)}, u32[]{:S(2)}) collective-permute-start(f32[4,2,32,128]{3,2,1,0:T(8,128)S(1)} %get-tuple-element.77), channel_id=1, source_target_pairs={{0,7},{1,6},{2,5},{3,4},{4,3},{5,2},{6,1},{7,0},{8,15},{9,14},{10,... | collective-permute-start | bytes 393224 | tf_op jit(solution)/shard_map/ppermute | solution.py:330
  133.5 19.9 %collective-permute-start.16 = (f32[4,2,32,128]{3,2,1,0:T(8,128)S(1)}, f32[4,2,32,128]{3,2,1,0:T(8,128)S(1)}, u32[]{:S(2)}, u32[]{:S(2)}) collective-permute-start(f32[4,2,32,128]{3,2,1,0:T(8,128)S(1)} %get-tuple-element.63), channel_id=1, source_target_pairs={{0,1},{1,0},{2,3},{3,2},{4,5},{5,4},{6,7},{7,6},{8,9},{9,8},{10,11... | collective-permute-start | bytes 393224 | tf_op jit(solution)/shard_map/ppermute | solution.py:330
  135.3 19.1 %collective-permute-start.17 = (f32[4,2,32,128]{3,2,1,0:T(8,128)S(1)}, f32[4,2,32,128]{3,2,1,0:T(8,128)S(1)}, u32[]{:S(2)}, u32[]{:S(2)}) collective-permute-start(f32[4,2,32,128]{3,2,1,0:T(8,128)S(1)} %get-tuple-element.64), channel_id=1, source_target_pairs={{0,2},{1,3},{2,0},{3,1},{4,6},{5,7},{6,4},{7,5},{8,10},{9,11},{10,... | collective-permute-start | bytes 393224 | tf_op jit(solution)/shard_map/ppermute | solution.py:330
  146.3 21.9 %collective-permute-start.18 = (f32[4,2,32,128]{3,2,1,0:T(8,128)}, f32[4,2,32,128]{3,2,1,0:T(8,128)S(1)}, u32[]{:S(2)}, u32[]{:S(2)}) collective-permute-start(f32[4,2,32,128]{3,2,1,0:T(8,128)} %get-tuple-element.65), channel_id=1, source_target_pairs={{0,3},{1,2},{2,1},{3,0},{4,7},{5,6},{6,5},{7,4},{8,11},{9,10},{10,... | collective-permute-start | bytes 393224 | tf_op jit(solution)/shard_map/ppermute | solution.py:330
  149.9 18.3 %collective-permute-start.19 = (f32[4,2,32,128]{3,2,1,0:T(8,128)}, f32[4,2,32,128]{3,2,1,0:T(8,128)S(1)}, u32[]{:S(2)}, u32[]{:S(2)}) collective-permute-start(f32[4,2,32,128]{3,2,1,0:T(8,128)} %get-tuple-element.66), channel_id=1, source_target_pairs={{0,4},{1,5},{2,6},{3,7},{4,0},{5,1},{6,2},{7,3},{8,12},{9,13},{10,... | collective-permute-start | bytes 393224 | tf_op jit(solution)/shard_map/ppermute | solution.py:330
  153.1 15.1 %collective-permute-start.20 = (f32[4,2,32,128]{3,2,1,0:T(8,128)}, f32[4,2,32,128]{3,2,1,0:T(8,128)S(1)}, u32[]{:S(2)}, u32[]{:S(2)}) collective-permute-start(f32[4,2,32,128]{3,2,1,0:T(8,128)} %get-tuple-element.67), channel_id=1, source_target_pairs={{0,5},{1,4},{2,7},{3,6},{4,1},{5,0},{6,3},{7,2},{8,13},{9,12},{10,... | collective-permute-start | bytes 393224 | tf_op jit(solution)/shard_map/ppermute | solution.py:330
  153.5 18.7 %collective-permute-start.21 = (f32[4,2,32,128]{3,2,1,0:T(8,128)}, f32[4,2,32,128]{3,2,1,0:T(8,128)S(1)}, u32[]{:S(2)}, u32[]{:S(2)}) collective-permute-start(f32[4,2,32,128]{3,2,1,0:T(8,128)} %get-tuple-element.68), channel_id=1, source_target_pairs={{0,6},{1,7},{2,4},{3,5},{4,2},{5,3},{6,0},{7,1},{8,14},{9,15},{10,... | collective-permute-start | bytes 393224 | tf_op jit(solution)/shard_map/ppermute | solution.py:330
  154.5 20.8 %collective-permute-start.22 = (f32[4,2,32,128]{3,2,1,0:T(8,128)}, f32[4,2,32,128]{3,2,1,0:T(8,128)S(1)}, u32[]{:S(2)}, u32[]{:S(2)}) collective-permute-start(f32[4,2,32,128]{3,2,1,0:T(8,128)} %copy-done.13), channel_id=1, source_target_pairs={{0,7},{1,6},{2,5},{3,4},{4,3},{5,2},{6,1},{7,0},{8,15},{9,14},{10,... | collective-permute-start | bytes 393224 | tf_op jit(solution)/shard_map/ppermute | solution.py:330
  (28 other events, 226.8 us)

commit v2 on v1

--- a/solution.py
+++ b/solution.py
@@ -103,7 +103,6 @@
             jax.ShapeDtypeStruct((2, size, size), F32),
             *[jax.ShapeDtypeStruct((2, size, width), F32)] * strips,
         ],
-        compiler_params=compiler_params(),
         name="prefixes",
     )(position, inverse_blocks, couplings, lead)
 
@@ -115,18 +114,20 @@
     sends = refs[-1 - n_energy : -1]
     green_ref, carried = refs[-2 - n_energy], refs[-1]
     rows, lanes = sends[0].shape[-2:]
+    columns = slice(strip * lanes, (strip + 1) * lanes)
 
     @pl.when(pl.program_id(0) == 0)
     def _():
         @pl.when(position[0] == 0)
         def _():
-            carried[...] = lead_ref[0, :, :, strip * lanes : (strip + 1) * lanes]
+            carried[...] = lead_ref[0, :, :, columns]
 
         for distance in range(1, n_slabs):
 
             @pl.when(position[0] == distance)
             def _():
-                carried[...] = firsts[distance - 1][...]
+                ref = firsts[distance - 1]
+                carried[...] = ref[...] if ref.shape[-1] == lanes else ref[:, :, columns]
 
         for distance in range(n_slabs - 2, 0, -1):
 
@@ -159,15 +160,14 @@
     blocks, _, size, _ = prefix.shape
     energies = lead.shape[0]
     rows = size // n_energy
-    lanes = firsts[0].shape[-1] if firsts else LANES
+    lanes = LANES
     n_slabs = len(firsts) + 1
     square = pl.BlockSpec((2, size, size), lambda k, s: (0, 0, 0))
-    narrow = pl.BlockSpec((2, size, lanes), lambda k, s: (0, 0, 0))
     in_specs = [
         pl.BlockSpec((1, 2, size, size), lambda k, s: (k, 0, 0, 0)),
         pl.BlockSpec((1, 2, size, size), lambda k, s: (energy, 0, 0, 0)),
         *[square] * len(products),
-        *[narrow] * len(firsts),
+        *[pl.BlockSpec(first.shape, lambda k, s: (0, 0, 0)) for first in firsts],
     ]
     operands = [prefix, lead, *products, *firsts]
     aliases = {}
@@ -296,7 +296,9 @@
     position = jnp.stack([lax.axis_index("slab"), lax.axis_index("energy")]).astype(jnp.int32)
     prefix, products, firsts = [], [], []
     for e in range(local):
-        p, last, *first = prefixes(position, inverse_blocks, couplings, lead_column, e, strips)
+        p, last, *first = prefixes(
+            position, inverse_blocks, couplings, lead_column, e, 1 if e else strips
+        )
         prefix.append(p)
         products.append(
             [
@@ -304,9 +306,9 @@
                 for d in range(1, n_slabs - 1)
             ]
         )
-        firsts.append(
-            [[lax.ppermute(one, "slab", [(0, d)]) for d in range(1, n_slabs)] for one in first]
-        )
+        firsts.append([])
+        for one in first:
+            firsts[e].append([lax.ppermute(one, "slab", [(0, d)]) for d in range(1, n_slabs)])
     mix = mixing_matrix(energy_index, w_table, local, n_energy)
     green = None
     gathered = [[None] * (local * n_energy) for _ in range(strips)]
@@ -317,7 +319,7 @@
                 prefix[e],
                 lead_column,
                 products[e],
-                firsts[e][strip],
+                firsts[e][min(strip, len(firsts[e]) - 1)],
                 e,
                 strip,
                 n_energy,

time: 179 us -> 178 us (level)
  the two profiles are of different devices: /device:TPU:17 before, /device:TPU:15 now
where the time goes in v2:
time: 178 us; the launch traced here: 177 us
  starting transfers between devices  59.7 us (34%)
  waiting for transfers between devices  58.1 us (33%)
  Pallas kernels  42.7 us (24%)
  local copies, waits for them, and re-layouts  14.8 us (8%)
    ppermute x28, starting transfers between devices, per_device(): received = lax.ppermute(received, 'energy', route)  44.7 us
    ppermute x28, waiting for transfers between devices, per_device(): received = lax.ppermute(received, 'energy', route)  37.7 us
    pallas_call x4, Pallas kernels, columns(): pl.pallas_call(functools.partial(column_kernel, n_slabs, n_energy, strip)...  20.7 us
    ppermute x9, waiting for transfers between devices, per_device(): lax.ppermute(one, 'slab', [(0, d)])  20.4 us
    pallas_call x2, Pallas kernels, prefixes(): pl.pallas_call(prefix_kernel, grid_spec=pltpu.PrefetchScalarGridSpec(num_...  14.8 us
    ppermute x9, starting transfers between devices, per_device(): lax.ppermute(one, 'slab', [(0, d)])  9.65 us
    unnamed x50, local copies, waits for them, and re-layouts  7.68 us
    pallas_call x2, Pallas kernels, convolve(): pl.pallas_call(functools.partial(convolve_kernel, energies), grid=(blocks...  6.68 us
  transfers between devices with their start and end apart: 41, of which 14 were waited for; matrix products, arithmetic and copies ran while one was open for 4% of the time, Pallas kernels for 18%

profile of v2, /device:TPU:15, one launch (start us, length us, event | category | flops | bytes accessed | tf_op | source)
XLA Modules:
  0.0 177.1 jit_solution(12453092540355730420)
XLA Ops:
  1.3 7.4 %prefixes.3 = (f32[4,2,256,256]{3,2,1,0:T(8,128)}, f32[2,256,256]{2,1,0:T(8,128)}, f32[2,256,128]{2,1,0:T(8,128)}, f32[2,256,128]{2,1,0:T(8,128)}) custom-call(s32[2]{0:T(128)} %pad_add_fusion.position.refs_0_, f32[2,4,2,256,256]{4,3,2,1,0:T(8,128)} %g_ref.3, f32[2,4,2,256,256]{4,3,2,1,0:T(8,128)} %h_ref.3, f32[2,2,256,256]{3,2,1,0:T(8,128)} %refs_2_.7), custom_call_target="tpu_custom_call" | custom-call | tf_op jit(solution)/shard_map/prefixes/pallas_call | solution.py:85
  17.6 6.0 %collective-permute-done.9.refs_7_ = f32[2,256,128]{2,1,0:T(8,128)S(1)} collective-permute-done((f32[2,256,128]{2,1,0:T(8,128)}, f32[2,256,128]{2,1,0:T(8,128)S(1)}, u32[]{:S(2)}, u32[]{:S(2)}) %collective-permute-start.9) | collective-permute-done | bytes 262176 | tf_op jit(solution)/shard_map/ppermute | solution.py:311
  25.6 7.4 %prefixes.2 = (f32[4,2,256,256]{3,2,1,0:T(8,128)}, f32[2,256,256]{2,1,0:T(8,128)}, f32[2,256,256]{2,1,0:T(8,128)}) custom-call(s32[2]{0:T(128)} %pad_add_fusion.position.refs_0_, f32[2,4,2,256,256]{4,3,2,1,0:T(8,128)} %g_ref.3, f32[2,4,2,256,256]{4,3,2,1,0:T(8,128)} %h_ref.3, f32[2,2,256,256]{3,2,1,0:T(8,128)} %refs_2_.7), custom_call_target="tpu_custom_call" | custom-call | tf_op jit(solution)/shard_map/prefixes/pallas_call | solution.py:85
  35.7 6.6 %collective-permute-done.12.refs_7_ = f32[2,256,128]{2,1,0:T(8,128)} collective-permute-done((f32[2,256,128]{2,1,0:T(8,128)}, f32[2,256,128]{2,1,0:T(8,128)}, u32[]{:S(2)}, u32[]{:S(2)}) %collective-permute-start.12) | collective-permute-done | bytes 262176 | tf_op jit(solution)/shard_map/ppermute | solution.py:311
  45.3 5.9 %columns.4 = (f32[2,4,2,256,256]{4,3,2,1,0:T(8,128)}, f32[4,2,32,128]{3,2,1,0:T(8,128)S(1)}, f32[4,2,32,128]{3,2,1,0:T(8,128)S(1)}, f32[4,2,32,128]{3,2,1,0:T(8,...) custom-call(s32[2]{0:T(128)S(1)} %copy-done.17, ...), custom_call_target="tpu_custom_call" | custom-call | tf_op jit(solution)/shard_map/columns/pallas_call | solution.py:178
  51.2 5.7 %columns.5 = (f32[2,4,2,256,256]{4,3,2,1,0:T(8,128)}, f32[4,2,32,128]{3,2,1,0:T(8,128)S(1)}, f32[4,2,32,128]{3,2,1,0:T(8,128)S(1)}, f32[4,2,32,128]{3,2,1,0:T(8,...) custom-call(s32[2]{0:T(128)S(1)} %copy-done.17, ...), custom_call_target="tpu_custom_call", output_to_operand_aliasing={{0}: (8, {})} | custom-call | tf_op jit(solution)/shard_map/columns/pallas_call | solution.py:178
  56.9 2.4 %collective-permute-start.13 = (f32[4,2,32,128]{3,2,1,0:T(8,128)S(1)}, f32[4,2,32,128]{3,2,1,0:T(8,128)S(1)}, u32[]{:S(2)}, u32[]{:S(2)}) collective-permute-start(f32[4,2,32,128]{3,2,1,0:T(8,128)S(1)} %get-tuple-element.61), channel_id=1, source_target_pairs={{0,1},{1,0},{2,3},{3,2},{4,5},{5,4},{6,7},{7,6},{8,9},{9,8},{10,11... | collective-permute-start | bytes 393224 | tf_op jit(solution)/shard_map/ppermute | solution.py:332
  59.4 2.1 %collective-permute-start.15 = (f32[4,2,32,128]{3,2,1,0:T(8,128)S(1)}, f32[4,2,32,128]{3,2,1,0:T(8,128)S(1)}, u32[]{:S(2)}, u32[]{:S(2)}) collective-permute-start(f32[4,2,32,128]{3,2,1,0:T(8,128)S(1)} %get-tuple-element.63), channel_id=1, source_target_pairs={{0,3},{1,2},{2,1},{3,0},{4,7},{5,6},{6,5},{7,4},{8,11},{9,10},{10,... | collective-permute-start | bytes 393224 | tf_op jit(solution)/shard_map/ppermute | solution.py:332
  61.5 2.3 %collective-permute-start.16 = (f32[4,2,32,128]{3,2,1,0:T(8,128)S(1)}, f32[4,2,32,128]{3,2,1,0:T(8,128)S(1)}, u32[]{:S(2)}, u32[]{:S(2)}) collective-permute-start(f32[4,2,32,128]{3,2,1,0:T(8,128)S(1)} %get-tuple-element.64), channel_id=1, source_target_pairs={{0,4},{1,5},{2,6},{3,7},{4,0},{5,1},{6,2},{7,3},{8,12},{9,13},{10,... | collective-permute-start | bytes 393224 | tf_op jit(solution)/shard_map/ppermute | solution.py:332
  63.8 7.7 %collective-permute-done.4.refs_7_ = f32[2,256,256]{2,1,0:T(8,128)S(1)} collective-permute-done((f32[2,256,256]{2,1,0:T(8,128)}, f32[2,256,256]{2,1,0:T(8,128)S(1)}, u32[]{:S(2)}, u32[]{:S(2)}) %collective-permute-start.4) | collective-permute-done | bytes 524320 | tf_op jit(solution)/shard_map/ppermute | solution.py:311
  71.6 4.9 %collective-permute-start.17 = (f32[4,2,32,128]{3,2,1,0:T(8,128)S(1)}, f32[4,2,32,128]{3,2,1,0:T(8,128)S(1)}, u32[]{:S(2)}, u32[]{:S(2)}) collective-permute-start(f32[4,2,32,128]{3,2,1,0:T(8,128)S(1)} %get-tuple-element.65), channel_id=1, source_target_pairs={{0,5},{1,4},{2,7},{3,6},{4,1},{5,0},{6,3},{7,2},{8,13},{9,12},{10,... | collective-permute-start | bytes 393224 | tf_op jit(solution)/shard_map/ppermute | solution.py:332
  76.4 4.6 %columns.6 = (f32[2,4,2,256,256]{4,3,2,1,0:T(8,128)}, f32[4,2,32,128]{3,2,1,0:T(8,128)S(1)}, f32[4,2,32,128]{3,2,1,0:T(8,128)S(1)}, f32[4,2,32,128]{3,2,1,0:T(8,...) custom-call(s32[2]{0:T(128)S(1)} %copy-done.17, ...), custom_call_target="tpu_custom_call", output_to_operand_aliasing={{0}: (8, {})} | custom-call | tf_op jit(solution)/shard_map/columns/pallas_call | solution.py:178
  81.0 4.5 %columns.7 = (f32[2,4,2,256,256]{4,3,2,1,0:T(8,128)}, f32[4,2,32,128]{3,2,1,0:T(8,128)S(1)}, f32[4,2,32,128]{3,2,1,0:T(8,128)S(1)}, f32[4,2,32,128]{3,2,1,0:T(8,...) custom-call(s32[2]{0:T(128)S(1)} %copy-done.17, ...), custom_call_target="tpu_custom_call", output_to_operand_aliasing={{0}: (8, {})} | custom-call | tf_op jit(solution)/shard_map/columns/pallas_call | solution.py:178
  86.4 1.8 collective-permute-start.20
  88.1 1.9 %collective-permute-start.21 = (f32[4,2,32,128]{3,2,1,0:T(8,128)S(1)}, f32[4,2,32,128]{3,2,1,0:T(8,128)S(1)}, u32[]{:S(2)}, u32[]{:S(2)}) collective-permute-start(f32[4,2,32,128]{3,2,1,0:T(8,128)S(1)} %get-tuple-element.70), channel_id=1, source_target_pairs={{0,2},{1,3},{2,0},{3,1},{4,6},{5,7},{6,4},{7,5},{8,10},{9,11},{10,... | collective-permute-start | bytes 393224 | tf_op jit(solution)/shard_map/ppermute | solution.py:332
  90.4 6.1 %collective-permute-done.18.refs_6_ = f32[4,2,32,128]{3,2,1,0:T(8,128)S(1)} collective-permute-done((f32[4,2,32,128]{3,2,1,0:T(8,128)S(1)}, f32[4,2,32,128]{3,2,1,0:T(8,128)S(1)}, u32[]{:S(2)}, u32[]{:S(2)}) %collective-permute-start.18) | collective-permute-done | bytes 131104 | tf_op jit(solution)/shard_map/ppermute | solution.py:332
  97.7 3.5 %collective-permute-start.30 = (f32[4,2,32,128]{3,2,1,0:T(8,128)S(1)}, f32[4,2,32,128]{3,2,1,0:T(8,128)S(1)}, u32[]{:S(2)}, u32[]{:S(2)}) collective-permute-start(f32[4,2,32,128]{3,2,1,0:T(8,128)S(1)} %get-tuple-element.80), channel_id=1, source_target_pairs={{0,4},{1,5},{2,6},{3,7},{4,0},{5,1},{6,2},{7,3},{8,12},{9,13},{10,... | collective-permute-start | bytes 393224 | tf_op jit(solution)/shard_map/ppermute | solution.py:332
  104.7 11.0 %collective-permute-done.30.refs_4_ = f32[4,2,32,128]{3,2,1,0:T(8,128)S(1)} collective-permute-done((f32[4,2,32,128]{3,2,1,0:T(8,128)S(1)}, f32[4,2,32,128]{3,2,1,0:T(8,128)S(1)}, u32[]{:S(2)}, u32[]{:S(2)}) %collective-permute-start.30) | collective-permute-done | bytes 131104 | tf_op jit(solution)/shard_map/ppermute | solution.py:332
  115.7 2.0 %collective-permute-start.35 = (f32[4,2,32,128]{3,2,1,0:T(8,128)S(1)}, f32[4,2,32,128]{3,2,1,0:T(8,128)S(1)}, u32[]{:S(2)}, u32[]{:S(2)}) collective-permute-start(f32[4,2,32,128]{3,2,1,0:T(8,128)S(1)} %get-tuple-element.86), channel_id=1, source_target_pairs={{0,2},{1,3},{2,0},{3,1},{4,6},{5,7},{6,4},{7,5},{8,10},{9,11},{10,... | collective-permute-start | bytes 393224 | tf_op jit(solution)/shard_map/ppermute | solution.py:332
  118.5 2.5 %collective-permute-start.36 = (f32[4,2,32,128]{3,2,1,0:T(8,128)}, f32[4,2,32,128]{3,2,1,0:T(8,128)S(1)}, u32[]{:S(2)}, u32[]{:S(2)}) collective-permute-start(f32[4,2,32,128]{3,2,1,0:T(8,128)} %get-tuple-element.87), channel_id=1, source_target_pairs={{0,3},{1,2},{2,1},{3,0},{4,7},{5,6},{6,5},{7,4},{8,11},{9,10},{10,... | collective-permute-start | bytes 393224 | tf_op jit(solution)/shard_map/ppermute | solution.py:332
  122.4 2.3 %collective-permute-done.33.refs_7_ = f32[4,2,32,128]{3,2,1,0:T(8,128)S(1)} collective-permute-done((f32[4,2,32,128]{3,2,1,0:T(8,128)S(1)}, f32[4,2,32,128]{3,2,1,0:T(8,128)S(1)}, u32[]{:S(2)}, u32[]{:S(2)}) %collective-permute-start.33) | collective-permute-done | bytes 131104 | tf_op jit(solution)/shard_map/ppermute | solution.py:332
  124.8 1.9 %collective-permute-start.39 = (f32[4,2,32,128]{3,2,1,0:T(8,128)}, f32[4,2,32,128]{3,2,1,0:T(8,128)S(1)}, u32[]{:S(2)}, u32[]{:S(2)}) collective-permute-start(f32[4,2,32,128]{3,2,1,0:T(8,128)} %get-tuple-element.90), channel_id=1, source_target_pairs={{0,6},{1,7},{2,4},{3,5},{4,2},{5,3},{6,0},{7,1},{8,14},{9,15},{10,... | collective-permute-start | bytes 393224 | tf_op jit(solution)/shard_map/ppermute | solution.py:332
  128.6 4.4 %collective-permute-start.22 = (f32[4,2,32,128]{3,2,1,0:T(8,128)}, f32[4,2,32,128]{3,2,1,0:T(8,128)S(1)}, u32[]{:S(2)}, u32[]{:S(2)}) collective-permute-start(f32[4,2,32,128]{3,2,1,0:T(8,128)} %copy-done.22), channel_id=1, source_target_pairs={{0,3},{1,2},{2,1},{3,0},{4,7},{5,6},{6,5},{7,4},{8,11},{9,10},{10,... | collective-permute-start | bytes 393224 | tf_op jit(solution)/shard_map/ppermute | solution.py:332
  132.9 5.4 %collective-permute-done.37.refs_12_ = f32[4,2,32,128]{3,2,1,0:T(8,128)S(1)} collective-permute-done((f32[4,2,32,128]{3,2,1,0:T(8,128)}, f32[4,2,32,128]{3,2,1,0:T(8,128)S(1)}, u32[]{:S(2)}, u32[]{:S(2)}) %collective-permute-start.37) | collective-permute-done | bytes 131104 | tf_op jit(solution)/shard_map/ppermute | solution.py:332
  138.3 3.0 %collective-permute-start.23 = (f32[4,2,32,128]{3,2,1,0:T(8,128)}, f32[4,2,32,128]{3,2,1,0:T(8,128)S(1)}, u32[]{:S(2)}, u32[]{:S(2)}) collective-permute-start(f32[4,2,32,128]{3,2,1,0:T(8,128)} %copy-done.21), channel_id=1, source_target_pairs={{0,4},{1,5},{2,6},{3,7},{4,0},{5,1},{6,2},{7,3},{8,12},{9,13},{10,... | collective-permute-start | bytes 393224 | tf_op jit(solution)/shard_map/ppermute | solution.py:332
  143.1 4.7 %collective-permute-start.24 = (f32[4,2,32,128]{3,2,1,0:T(8,128)}, f32[4,2,32,128]{3,2,1,0:T(8,128)S(1)}, u32[]{:S(2)}, u32[]{:S(2)}) collective-permute-start(f32[4,2,32,128]{3,2,1,0:T(8,128)} %copy-done.20), channel_id=1, source_target_pairs={{0,5},{1,4},{2,7},{3,6},{4,1},{5,0},{6,3},{7,2},{8,13},{9,12},{10,... | collective-permute-start | bytes 393224 | tf_op jit(solution)/shard_map/ppermute | solution.py:332
  150.2 2.1 %collective-permute-start.25 = (f32[4,2,32,128]{3,2,1,0:T(8,128)}, f32[4,2,32,128]{3,2,1,0:T(8,128)S(1)}, u32[]{:S(2)}, u32[]{:S(2)}) collective-permute-start(f32[4,2,32,128]{3,2,1,0:T(8,128)} %copy-done.19), channel_id=1, source_target_pairs={{0,6},{1,7},{2,4},{3,5},{4,2},{5,3},{6,0},{7,1},{8,14},{9,15},{10,... | collective-permute-start | bytes 393224 | tf_op jit(solution)/shard_map/ppermute | solution.py:332
  152.3 7.1 %collective-permute-done.40.refs_15_ = f32[4,2,32,128]{3,2,1,0:T(8,128)} collective-permute-done((f32[4,2,32,128]{3,2,1,0:T(8,128)}, f32[4,2,32,128]{3,2,1,0:T(8,128)}, u32[]{:S(2)}, u32[]{:S(2)}) %collective-permute-start.40) | collective-permute-done | bytes 131104 | tf_op jit(solution)/shard_map/ppermute | solution.py:332
  160.6 2.1 %gather_fusion.1 = f32[256]{0:T(256)S(1)} fusion(f32[16383]{0:T(1024)} %bitcast.10, s32[1024]{0:T(1024)S(1)} %pad_clamp_fusion), kind=kCustom, calls=%fused_computation.1 | custom fusion | bytes 3072 | tf_op jit(solution)/shard_map/gather | solution.py:240
  162.8 2.7 %gather_fusion.2 = f32[256]{0:T(256)} fusion(f32[16383]{0:T(1024)} %bitcast.9, s32[1024]{0:T(1024)S(1)} %pad_clamp_fusion), kind=kCustom, calls=%fused_computation.2 | custom fusion | bytes 3072 | tf_op jit(solution)/shard_map/gather | solution.py:240
  170.3 3.9 %convolve.2.refs_16_ = f32[16,4,2,32,256]{4,3,2,1,0:T(8,128)} custom-call(bf16[256,256]{1,0:T(8,128)(2,1)S(1)} %get-tuple-element.58.high_ref, bf16[256,256]{1,0:T(8,128)(2,1)S(1)} %get-tuple-element.59.low_ref, f32[4,2,32,128]{3,2,1,0:T(8,128)S(1)} %copy-done.8, f32[4,2,32,128]{3,2,1,0:T(8,128)S(1)} %collective-permute-done.27.refs_1_, ...), custom_call_target="tpu_custom_call" | custom-call | tf_op jit(solution)/shard_map/convolve/pallas_call | solution.py:279
  174.2 2.8 %convolve.3 = f32[16,4,2,32,256]{4,3,2,1,0:T(8,128)} custom-call(bf16[256,256]{1,0:T(8,128)(2,1)S(1)} %get-tuple-element.58.high_ref, bf16[256,256]{1,0:T(8,128)(2,1)S(1)} %get-tuple-element.59.low_ref, f32[4,2,32,128]{3,2,1,0:T(8,128)S(1)} %get-tuple-element.60.refs_0_, ...), custom_call_target="tpu_custom_call", output_to_operand_aliasing={{}: (18, {})} | custom-call | tf_op jit(solution)/shard_map/convolve/pallas_call | solution.py:279
  (124 shorter events, 37.5 us)
Async XLA Ops:
  10.0 13.5 %collective-permute-start.9 = (f32[2,256,128]{2,1,0:T(8,128)}, f32[2,256,128]{2,1,0:T(8,128)S(1)}, u32[]{:S(2)}, u32[]{:S(2)}) collective-permute-start(f32[2,256,128]{2,1,0:T(8,128)} %get-tuple-element.52), channel_id=1, source_target_pairs={{0,24},{1,25},{2,26},{3,27},{4,28},{5,29},{6,30},{7,31}} | collective-permute-start | bytes 786440 | tf_op jit(solution)/shard_map/ppermute | solution.py:311
  11.3 31.7 %collective-permute-start.5 = (f32[2,256,256]{2,1,0:T(8,128)}, f32[2,256,256]{2,1,0:T(8,128)}, u32[]{:S(2)}, u32[]{:S(2)}) collective-permute-start(f32[2,256,256]{2,1,0:T(8,128)} %get-tuple-element.51), channel_id=1, source_target_pairs={{8,16},{16,24},{9,17},{17,25},{10,18},{18,26},{11,19},{19,27},{12,... | collective-permute-start | bytes 1572872 | tf_op jit(solution)/shard_map/ppermute | solution.py:305
  12.6 31.2 %collective-permute-start.6 = (f32[2,256,256]{2,1,0:T(8,128)}, f32[2,256,256]{2,1,0:T(8,128)}, u32[]{:S(2)}, u32[]{:S(2)}) collective-permute-start(f32[2,256,256]{2,1,0:T(8,128)} %get-tuple-element.51), channel_id=1, source_target_pairs={{8,24},{9,25},{10,26},{11,27},{12,28},{13,29},{14,30},{15,31}} | collective-permute-start | bytes 1572872 | tf_op jit(solution)/shard_map/ppermute | solution.py:305
  14.0 19.0 %collective-permute-start.10 = (f32[2,256,128]{2,1,0:T(8,128)}, f32[2,256,128]{2,1,0:T(8,128)}, u32[]{:S(2)}, u32[]{:S(2)}) collective-permute-start(f32[2,256,128]{2,1,0:T(8,128)} %get-tuple-element.53), channel_id=1, source_target_pairs={{0,8},{1,9},{2,10},{3,11},{4,12},{5,13},{6,14},{7,15}} | collective-permute-start | bytes 786440 | tf_op jit(solution)/shard_map/ppermute | solution.py:311
  16.2 18.2 %collective-permute-start.11 = (f32[2,256,128]{2,1,0:T(8,128)}, f32[2,256,128]{2,1,0:T(8,128)}, u32[]{:S(2)}, u32[]{:S(2)}) collective-permute-start(f32[2,256,128]{2,1,0:T(8,128)} %get-tuple-element.53), channel_id=1, source_target_pairs={{0,16},{1,17},{2,18},{3,19},{4,20},{5,21},{6,22},{7,23}} | collective-permute-start | bytes 786440 | tf_op jit(solution)/shard_map/ppermute | solution.py:311
  24.3 18.1 %collective-permute-start.12 = (f32[2,256,128]{2,1,0:T(8,128)}, f32[2,256,128]{2,1,0:T(8,128)}, u32[]{:S(2)}, u32[]{:S(2)}) collective-permute-start(f32[2,256,128]{2,1,0:T(8,128)} %get-tuple-element.53), channel_id=1, source_target_pairs={{0,24},{1,25},{2,26},{3,27},{4,28},{5,29},{6,30},{7,31}} | collective-permute-start | bytes 786440 | tf_op jit(solution)/shard_map/ppermute | solution.py:311
  33.0 23.9 %collective-permute-start = (f32[2,256,256]{2,1,0:T(8,128)}, f32[2,256,256]{2,1,0:T(8,128)S(1)}, u32[]{:S(2)}, u32[]{:S(2)}) collective-permute-start(f32[2,256,256]{2,1,0:T(8,128)} %get-tuple-element.48), channel_id=1, source_target_pairs={{8,16},{16,24},{9,17},{17,25},{10,18},{18,26},{11,19},{19,27},{12,... | collective-permute-start | bytes 1572872 | tf_op jit(solution)/shard_map/ppermute | solution.py:305
  34.4 24.8 %collective-permute-start.1 = (f32[2,256,256]{2,1,0:T(8,128)}, f32[2,256,256]{2,1,0:T(8,128)S(1)}, u32[]{:S(2)}, u32[]{:S(2)}) collective-permute-start(f32[2,256,256]{2,1,0:T(8,128)} %get-tuple-element.48), channel_id=1, source_target_pairs={{8,24},{9,25},{10,26},{11,27},{12,28},{13,29},{14,30},{15,31}} | collective-permute-start | bytes 1572872 | tf_op jit(solution)/shard_map/ppermute | solution.py:305
  42.4 17.0 %collective-permute-start.2 = (f32[2,256,256]{2,1,0:T(8,128)}, f32[2,256,256]{2,1,0:T(8,128)S(1)}, u32[]{:S(2)}, u32[]{:S(2)}) collective-permute-start(f32[2,256,256]{2,1,0:T(8,128)} %get-tuple-element.49), channel_id=1, source_target_pairs={{0,8},{1,9},{2,10},{3,11},{4,12},{5,13},{6,14},{7,15}} | collective-permute-start | bytes 1572872 | tf_op jit(solution)/shard_map/ppermute | solution.py:311
  43.1 18.4 %collective-permute-start.3 = (f32[2,256,256]{2,1,0:T(8,128)}, f32[2,256,256]{2,1,0:T(8,128)S(1)}, u32[]{:S(2)}, u32[]{:S(2)}) collective-permute-start(f32[2,256,256]{2,1,0:T(8,128)} %get-tuple-element.49), channel_id=1, source_target_pairs={{0,16},{1,17},{2,18},{3,19},{4,20},{5,21},{6,22},{7,23}} | collective-permute-start | bytes 1572872 | tf_op jit(solution)/shard_map/ppermute | solution.py:311
  43.8 27.8 %collective-permute-start.4 = (f32[2,256,256]{2,1,0:T(8,128)}, f32[2,256,256]{2,1,0:T(8,128)S(1)}, u32[]{:S(2)}, u32[]{:S(2)}) collective-permute-start(f32[2,256,256]{2,1,0:T(8,128)} %get-tuple-element.49), channel_id=1, source_target_pairs={{0,24},{1,25},{2,26},{3,27},{4,28},{5,29},{6,30},{7,31}} | collective-permute-start | bytes 1572872 | tf_op jit(solution)/shard_map/ppermute | solution.py:311
  56.9 29.3 %collective-permute-start.13 = (f32[4,2,32,128]{3,2,1,0:T(8,128)S(1)}, f32[4,2,32,128]{3,2,1,0:T(8,128)S(1)}, u32[]{:S(2)}, u32[]{:S(2)}) collective-permute-start(f32[4,2,32,128]{3,2,1,0:T(8,128)S(1)} %get-tuple-element.61), channel_id=1, source_target_pairs={{0,1},{1,0},{2,3},{3,2},{4,5},{5,4},{6,7},{7,6},{8,9},{9,8},{10,11... | collective-permute-start | bytes 393224 | tf_op jit(solution)/shard_map/ppermute | solution.py:332
  59.3 27.0 %collective-permute-start.14 = (f32[4,2,32,128]{3,2,1,0:T(8,128)S(1)}, f32[4,2,32,128]{3,2,1,0:T(8,128)S(1)}, u32[]{:S(2)}, u32[]{:S(2)}) collective-permute-start(f32[4,2,32,128]{3,2,1,0:T(8,128)S(1)} %get-tuple-element.62), channel_id=1, source_target_pairs={{0,2},{1,3},{2,0},{3,1},{4,6},{5,7},{6,4},{7,5},{8,10},{9,11},{10,... | collective-permute-start | bytes 393224 | tf_op jit(solution)/shard_map/ppermute | solution.py:332
  59.4 26.9 %collective-permute-start.15 = (f32[4,2,32,128]{3,2,1,0:T(8,128)S(1)}, f32[4,2,32,128]{3,2,1,0:T(8,128)S(1)}, u32[]{:S(2)}, u32[]{:S(2)}) collective-permute-start(f32[4,2,32,128]{3,2,1,0:T(8,128)S(1)} %get-tuple-element.63), channel_id=1, source_target_pairs={{0,3},{1,2},{2,1},{3,0},{4,7},{5,6},{6,5},{7,4},{8,11},{9,10},{10,... | collective-permute-start | bytes 393224 | tf_op jit(solution)/shard_map/ppermute | solution.py:332
  61.5 26.7 %collective-permute-start.16 = (f32[4,2,32,128]{3,2,1,0:T(8,128)S(1)}, f32[4,2,32,128]{3,2,1,0:T(8,128)S(1)}, u32[]{:S(2)}, u32[]{:S(2)}) collective-permute-start(f32[4,2,32,128]{3,2,1,0:T(8,128)S(1)} %get-tuple-element.64), channel_id=1, source_target_pairs={{0,4},{1,5},{2,6},{3,7},{4,0},{5,1},{6,2},{7,3},{8,12},{9,13},{10,... | collective-permute-start | bytes 393224 | tf_op jit(solution)/shard_map/ppermute | solution.py:332
  71.6 18.5 %collective-permute-start.17 = (f32[4,2,32,128]{3,2,1,0:T(8,128)S(1)}, f32[4,2,32,128]{3,2,1,0:T(8,128)S(1)}, u32[]{:S(2)}, u32[]{:S(2)}) collective-permute-start(f32[4,2,32,128]{3,2,1,0:T(8,128)S(1)} %get-tuple-element.65), channel_id=1, source_target_pairs={{0,5},{1,4},{2,7},{3,6},{4,1},{5,0},{6,3},{7,2},{8,13},{9,12},{10,... | collective-permute-start | bytes 393224 | tf_op jit(solution)/shard_map/ppermute | solution.py:332
  86.3 11.4 %collective-permute-start.19 = (f32[4,2,32,128]{3,2,1,0:T(8,128)S(1)}, f32[4,2,32,128]{3,2,1,0:T(8,128)S(1)}, u32[]{:S(2)}, u32[]{:S(2)}) collective-permute-start(f32[4,2,32,128]{3,2,1,0:T(8,128)S(1)} %get-tuple-element.67), channel_id=1, source_target_pairs={{0,7},{1,6},{2,5},{3,4},{4,3},{5,2},{6,1},{7,0},{8,15},{9,14},{10,... | collective-permute-start | bytes 393224 | tf_op jit(solution)/shard_map/ppermute | solution.py:332
  88.1 13.1 %collective-permute-start.21 = (f32[4,2,32,128]{3,2,1,0:T(8,128)S(1)}, f32[4,2,32,128]{3,2,1,0:T(8,128)S(1)}, u32[]{:S(2)}, u32[]{:S(2)}) collective-permute-start(f32[4,2,32,128]{3,2,1,0:T(8,128)S(1)} %get-tuple-element.70), channel_id=1, source_target_pairs={{0,2},{1,3},{2,0},{3,1},{4,6},{5,7},{6,4},{7,5},{8,10},{9,11},{10,... | collective-permute-start | bytes 393224 | tf_op jit(solution)/shard_map/ppermute | solution.py:332
  97.7 18.0 %collective-permute-start.30 = (f32[4,2,32,128]{3,2,1,0:T(8,128)S(1)}, f32[4,2,32,128]{3,2,1,0:T(8,128)S(1)}, u32[]{:S(2)}, u32[]{:S(2)}) collective-permute-start(f32[4,2,32,128]{3,2,1,0:T(8,128)S(1)} %get-tuple-element.80), channel_id=1, source_target_pairs={{0,4},{1,5},{2,6},{3,7},{4,0},{5,1},{6,2},{7,3},{8,12},{9,13},{10,... | collective-permute-start | bytes 393224 | tf_op jit(solution)/shard_map/ppermute | solution.py:332
  101.2 17.3 %collective-permute-start.31 = (f32[4,2,32,128]{3,2,1,0:T(8,128)S(1)}, f32[4,2,32,128]{3,2,1,0:T(8,128)S(1)}, u32[]{:S(2)}, u32[]{:S(2)}) collective-permute-start(f32[4,2,32,128]{3,2,1,0:T(8,128)S(1)} %get-tuple-element.81), channel_id=1, source_target_pairs={{0,5},{1,4},{2,7},{3,6},{4,1},{5,0},{6,3},{7,2},{8,13},{9,12},{10,... | collective-permute-start | bytes 393224 | tf_op jit(solution)/shard_map/ppermute | solution.py:332
  101.5 20.9 %collective-permute-start.32 = (f32[4,2,32,128]{3,2,1,0:T(8,128)S(1)}, f32[4,2,32,128]{3,2,1,0:T(8,128)S(1)}, u32[]{:S(2)}, u32[]{:S(2)}) collective-permute-start(f32[4,2,32,128]{3,2,1,0:T(8,128)S(1)} %get-tuple-element.82), channel_id=1, source_target_pairs={{0,6},{1,7},{2,4},{3,5},{4,2},{5,3},{6,0},{7,1},{8,14},{9,15},{10,... | collective-permute-start | bytes 393224 | tf_op jit(solution)/shard_map/ppermute | solution.py:332
  102.7 22.0 %collective-permute-start.33 = (f32[4,2,32,128]{3,2,1,0:T(8,128)S(1)}, f32[4,2,32,128]{3,2,1,0:T(8,128)S(1)}, u32[]{:S(2)}, u32[]{:S(2)}) collective-permute-start(f32[4,2,32,128]{3,2,1,0:T(8,128)S(1)} %get-tuple-element.83), channel_id=1, source_target_pairs={{0,7},{1,6},{2,5},{3,4},{4,3},{5,2},{6,1},{7,0},{8,15},{9,14},{10,... | collective-permute-start | bytes 393224 | tf_op jit(solution)/shard_map/ppermute | solution.py:332
  103.8 21.0 %collective-permute-start.34 = (f32[4,2,32,128]{3,2,1,0:T(8,128)S(1)}, f32[4,2,32,128]{3,2,1,0:T(8,128)S(1)}, u32[]{:S(2)}, u32[]{:S(2)}) collective-permute-start(f32[4,2,32,128]{3,2,1,0:T(8,128)S(1)} %get-tuple-element.85), channel_id=1, source_target_pairs={{0,1},{1,0},{2,3},{3,2},{4,5},{5,4},{6,7},{7,6},{8,9},{9,8},{10,11... | collective-permute-start | bytes 393224 | tf_op jit(solution)/shard_map/ppermute | solution.py:332
  122.4 15.9 %collective-permute-start.37 = (f32[4,2,32,128]{3,2,1,0:T(8,128)}, f32[4,2,32,128]{3,2,1,0:T(8,128)S(1)}, u32[]{:S(2)}, u32[]{:S(2)}) collective-permute-start(f32[4,2,32,128]{3,2,1,0:T(8,128)} %get-tuple-element.88), channel_id=1, source_target_pairs={{0,4},{1,5},{2,6},{3,7},{4,0},{5,1},{6,2},{7,3},{8,12},{9,13},{10,... | collective-permute-start | bytes 393224 | tf_op jit(solution)/shard_map/ppermute | solution.py:332
  124.7 17.8 %collective-permute-start.38 = (f32[4,2,32,128]{3,2,1,0:T(8,128)}, f32[4,2,32,128]{3,2,1,0:T(8,128)S(1)}, u32[]{:S(2)}, u32[]{:S(2)}) collective-permute-start(f32[4,2,32,128]{3,2,1,0:T(8,128)} %get-tuple-element.89), channel_id=1, source_target_pairs={{0,5},{1,4},{2,7},{3,6},{4,1},{5,0},{6,3},{7,2},{8,13},{9,12},{10,... | collective-permute-start | bytes 393224 | tf_op jit(solution)/shard_map/ppermute | solution.py:332
  124.8 24.8 %collective-permute-start.39 = (f32[4,2,32,128]{3,2,1,0:T(8,128)}, f32[4,2,32,128]{3,2,1,0:T(8,128)S(1)}, u32[]{:S(2)}, u32[]{:S(2)}) collective-permute-start(f32[4,2,32,128]{3,2,1,0:T(8,128)} %get-tuple-element.90), channel_id=1, source_target_pairs={{0,6},{1,7},{2,4},{3,5},{4,2},{5,3},{6,0},{7,1},{8,14},{9,15},{10,... | collective-permute-start | bytes 393224 | tf_op jit(solution)/shard_map/ppermute | solution.py:332
  126.7 32.7 %collective-permute-start.40 = (f32[4,2,32,128]{3,2,1,0:T(8,128)}, f32[4,2,32,128]{3,2,1,0:T(8,128)}, u32[]{:S(2)}, u32[]{:S(2)}) collective-permute-start(f32[4,2,32,128]{3,2,1,0:T(8,128)} %get-tuple-element.91), channel_id=1, source_target_pairs={{0,7},{1,6},{2,5},{3,4},{4,3},{5,2},{6,1},{7,0},{8,15},{9,14},{10,... | collective-permute-start | bytes 393224 | tf_op jit(solution)/shard_map/ppermute | solution.py:332
  128.6 45.6 %collective-permute-start.22 = (f32[4,2,32,128]{3,2,1,0:T(8,128)}, f32[4,2,32,128]{3,2,1,0:T(8,128)S(1)}, u32[]{:S(2)}, u32[]{:S(2)}) collective-permute-start(f32[4,2,32,128]{3,2,1,0:T(8,128)} %copy-done.22), channel_id=1, source_target_pairs={{0,3},{1,2},{2,1},{3,0},{4,7},{5,6},{6,5},{7,4},{8,11},{9,10},{10,... | collective-permute-start | bytes 393224 | tf_op jit(solution)/shard_map/ppermute | solution.py:332
  138.3 35.9 %collective-permute-start.23 = (f32[4,2,32,128]{3,2,1,0:T(8,128)}, f32[4,2,32,128]{3,2,1,0:T(8,128)S(1)}, u32[]{:S(2)}, u32[]{:S(2)}) collective-permute-start(f32[4,2,32,128]{3,2,1,0:T(8,128)} %copy-done.21), channel_id=1, source_target_pairs={{0,4},{1,5},{2,6},{3,7},{4,0},{5,1},{6,2},{7,3},{8,12},{9,13},{10,... | collective-permute-start | bytes 393224 | tf_op jit(solution)/shard_map/ppermute | solution.py:332
  143.1 31.1 %collective-permute-start.24 = (f32[4,2,32,128]{3,2,1,0:T(8,128)}, f32[4,2,32,128]{3,2,1,0:T(8,128)S(1)}, u32[]{:S(2)}, u32[]{:S(2)}) collective-permute-start(f32[4,2,32,128]{3,2,1,0:T(8,128)} %copy-done.20), channel_id=1, source_target_pairs={{0,5},{1,4},{2,7},{3,6},{4,1},{5,0},{6,3},{7,2},{8,13},{9,12},{10,... | collective-permute-start | bytes 393224 | tf_op jit(solution)/shard_map/ppermute | solution.py:332
  150.2 24.0 %collective-permute-start.25 = (f32[4,2,32,128]{3,2,1,0:T(8,128)}, f32[4,2,32,128]{3,2,1,0:T(8,128)S(1)}, u32[]{:S(2)}, u32[]{:S(2)}) collective-permute-start(f32[4,2,32,128]{3,2,1,0:T(8,128)} %copy-done.19), channel_id=1, source_target_pairs={{0,6},{1,7},{2,4},{3,5},{4,2},{5,3},{6,0},{7,1},{8,14},{9,15},{10,... | collective-permute-start | bytes 393224 | tf_op jit(solution)/shard_map/ppermute | solution.py:332
  159.4 14.8 %collective-permute-start.26 = (f32[4,2,32,128]{3,2,1,0:T(8,128)}, f32[4,2,32,128]{3,2,1,0:T(8,128)S(1)}, u32[]{:S(2)}, u32[]{:S(2)}) collective-permute-start(f32[4,2,32,128]{3,2,1,0:T(8,128)} %copy-done.18), channel_id=1, source_target_pairs={{0,7},{1,6},{2,5},{3,4},{4,3},{5,2},{6,1},{7,0},{8,15},{9,14},{10,... | collective-permute-start | bytes 393224 | tf_op jit(solution)/shard_map/ppermute | solution.py:332
  (34 other events, 519.8 us)
